TPU v7x, 32 devices: a whole 2x2x4 slice. The times are simulated.
32 devices in a mesh: wide: 8 (over z, y), narrow: 4 (over x, core).
Axes of the slice: x: 2, y: 2, z: 4, core: 2. Of those that a mesh axis runs over, the one named last changes fastest.
Arguments:
- frames: bfloat16 [32, 512, 1024], P(('wide', 'narrow')), may hold values from -6 to 6
- lengths: int32 [32], P(('wide', 'narrow')), may hold values from 64 to 512, as said below
- w_query: bfloat16 [1024, 1024], P(('wide', 'narrow')), may hold values from -0.25 to 0.25
- w_key: bfloat16 [1024, 1024], P(('wide', 'narrow')), may hold values from -0.25 to 0.25
- w_value: bfloat16 [1024, 1024], P(('wide', 'narrow')), may hold values from -0.1875 to 0.1875
- w_out: bfloat16 [1024, 1024], P(('wide', 'narrow')), may hold values from -1 to 1
- w_up: bfloat16 [1024, 4096], P(('wide', 'narrow')), may hold values from -0.1875 to 0.1875
- w_down: bfloat16 [4096, 1024], P(('wide', 'narrow')), may hold values from -0.09375 to 0.09375
- gain_attn: bfloat16 [1024], P(('wide', 'narrow')), may hold values from 0.099609375 to 1.8984375
- gain_mlp: bfloat16 [1024], P(('wide', 'narrow')), may hold values from 0.099609375 to 1.8984375
- cotangent: bfloat16 [32, 512, 1024], P(('wide', 'narrow')), may hold values from -6 to 6
Outputs:
- output: bfloat16 [32, 512, 1024], P(('wide', 'narrow'))
- grad_frames: float32 [32, 512, 1024], P(('wide', 'narrow'))
- grad_query: float32 [1024, 1024], P(('wide', 'narrow'))
- grad_key: float32 [1024, 1024], P(('wide', 'narrow'))
- grad_value: float32 [1024, 1024], P(('wide', 'narrow'))
- grad_out: float32 [1024, 1024], P(('wide', 'narrow'))
- grad_up: float32 [1024, 4096], P(('wide', 'narrow'))
- grad_down: float32 [4096, 1024], P(('wide', 'narrow'))
- grad_gain_attn: float32 [1024], P(('wide', 'narrow'))
- grad_gain_mlp: float32 [1024], P(('wide', 'narrow'))
Inputs may be any that keep to these rules, and one draw needn't show every extreme that they name: `lengths`: every draw has an item of exactly 512 frames and one of exactly 64.
All inputs are finite; a program needn't handle non-finite values.
Results may differ from a plain program's by a relative error of at most 0.013.
The roundings to bfloat16 on the way count: a program that leaves them out, or rounds other values in their place, can miss the bound.
Values may be sent and summed in bfloat16 or wider, within the bound.
No kernel may reach another device: no remote copies, remote signals or barrier semaphores. Data moves between devices by JAX's collectives and lax.ppermute only.
A program may use at most 256 MiB of HBM per device.

v0:
```python
from functools import partial

import jax
import jax.numpy as jnp
from jax import lax
from jax.sharding import PartitionSpec as P

HEADS = 16
HEAD_DIM = 64


EPSILON = 1e-06


def norm_forward(rows_in, gain):
    inverse = lax.rsqrt(jnp.mean(rows_in * rows_in, axis=-1, keepdims=True) + EPSILON)
    normal = rows_in * inverse
    return (normal * gain, normal, inverse)


def norm_backward(grad_in, gain, normal, inverse):
    scaled = grad_in * gain
    grad_rows = inverse * (scaled - normal * jnp.mean(scaled * normal, axis=-1, keepdims=True))
    return (grad_rows, jnp.sum(grad_in * normal, axis=0))


def fetch_weights(w_query, w_key, w_value, w_out, w_up, w_down, gain_attn, gain_mlp):
    return (
        lax.all_gather(w_query, ("wide", "narrow"), axis=0, tiled=True),
        lax.all_gather(w_key, ("wide", "narrow"), axis=0, tiled=True),
        lax.all_gather(w_value, ("wide", "narrow"), axis=0, tiled=True),
        lax.all_gather(w_out, ("wide", "narrow"), axis=0, tiled=True),
        lax.all_gather(w_up, ("wide", "narrow"), axis=0, tiled=True),
        lax.all_gather(w_down, ("wide", "narrow"), axis=0, tiled=True),
        lax.all_gather(gain_attn, ("wide", "narrow"), axis=0, tiled=True),
        lax.all_gather(gain_mlp, ("wide", "narrow"), axis=0, tiled=True),
    )


def spread_grads(
    grad_query, grad_key, grad_value, grad_outmat, grad_up, grad_down, grad_gain1, grad_gain2
):
    return (
        lax.psum_scatter(grad_query, ("wide", "narrow"), scatter_dimension=0, tiled=True),
        lax.psum_scatter(grad_key, ("wide", "narrow"), scatter_dimension=0, tiled=True),
        lax.psum_scatter(grad_value, ("wide", "narrow"), scatter_dimension=0, tiled=True),
        lax.psum_scatter(grad_outmat, ("wide", "narrow"), scatter_dimension=0, tiled=True),
        lax.psum_scatter(grad_up, ("wide", "narrow"), scatter_dimension=0, tiled=True),
        lax.psum_scatter(grad_down, ("wide", "narrow"), scatter_dimension=0, tiled=True),
        lax.psum_scatter(grad_gain1, ("wide", "narrow"), scatter_dimension=0, tiled=True),
        lax.psum_scatter(grad_gain2, ("wide", "narrow"), scatter_dimension=0, tiled=True),
    )


def masked_scores(queries, key_rows, key_mask):
    factor = HEAD_DIM ** (-0.5)
    scores = (
        jnp.einsum("qhd,khd->hqk", queries, key_rows, preferred_element_type=jnp.float32) * factor
    )
    return jnp.where(key_mask[None, None, :], scores, -1e30)


def attend(element):
    queries, key_rows, values, key_mask = element
    scores = masked_scores(queries, key_rows, key_mask)
    peak_score = jnp.max(scores, axis=-1, keepdims=True)
    expon = jnp.exp(scores - peak_score)
    totals = jnp.sum(expon, axis=-1, keepdims=True)
    shares = (expon / totals).astype(jnp.bfloat16)
    mixed = jnp.einsum("hqk,khd->qhd", shares, values, preferred_element_type=jnp.float32)
    return (mixed, peak_score + jnp.log(totals))


def attend_back(element):
    queries, key_rows, values, key_mask, log_total, grad_mixed = element
    factor = HEAD_DIM ** (-0.5)
    scores = masked_scores(queries, key_rows, key_mask)
    chance = jnp.exp(scores - log_total)
    grad_values = jnp.einsum(
        "hqk,qhd->khd", chance.astype(jnp.bfloat16), grad_mixed, preferred_element_type=jnp.float32
    )
    grad_chance = jnp.einsum("qhd,khd->hqk", grad_mixed, values, preferred_element_type=jnp.float32)
    grad_scores = (
        chance * (grad_chance - jnp.sum(chance * grad_chance, axis=-1, keepdims=True))
    ).astype(jnp.bfloat16)
    grad_queries = (
        jnp.einsum("hqk,khd->qhd", grad_scores, key_rows, preferred_element_type=jnp.float32)
        * factor
    )
    grad_keys = (
        jnp.einsum("hqk,qhd->khd", grad_scores, queries, preferred_element_type=jnp.float32)
        * factor
    )
    return (
        grad_queries.astype(jnp.bfloat16),
        grad_keys.astype(jnp.bfloat16),
        grad_values.astype(jnp.bfloat16),
    )


def recompute(frames, key_mask, row_mask, gathered):
    query_mat, key_mat, value_mat, out_mat, up_mat, down_mat, attn_gain, mlp_gain = gathered
    item_count, slot_len, model_width = frames.shape
    rows_in = frames.reshape(item_count * slot_len, model_width).astype(jnp.float32)
    normed_one, normal1, inverse1 = norm_forward(rows_in, attn_gain.astype(jnp.float32))
    hidden = normed_one.astype(jnp.bfloat16)
    split_shape = (item_count, slot_len, HEADS, HEAD_DIM)
    queries = (
        jnp.dot(hidden, query_mat, preferred_element_type=jnp.float32)
        .astype(jnp.bfloat16)
        .reshape(split_shape)
    )
    key_rows = (
        jnp.dot(hidden, key_mat, preferred_element_type=jnp.float32)
        .astype(jnp.bfloat16)
        .reshape(split_shape)
    )
    values = (
        jnp.dot(hidden, value_mat, preferred_element_type=jnp.float32)
        .astype(jnp.bfloat16)
        .reshape(split_shape)
    )
    mixed, log_total = lax.map(attend, (queries, key_rows, values, key_mask))
    mixed_low = mixed.reshape(item_count * slot_len, model_width).astype(jnp.bfloat16)
    middle = rows_in + jnp.dot(mixed_low, out_mat, preferred_element_type=jnp.float32)
    normed_two, normal2, inverse2 = norm_forward(middle, mlp_gain.astype(jnp.float32))
    second = normed_two.astype(jnp.bfloat16)
    upward = jnp.dot(second, up_mat, preferred_element_type=jnp.float32)
    active = jax.nn.gelu(upward, approximate=True).astype(jnp.bfloat16)
    result = (middle + jnp.dot(active, down_mat, preferred_element_type=jnp.float32)) * row_mask
    return (
        hidden,
        queries,
        key_rows,
        values,
        log_total,
        mixed_low,
        normal1,
        inverse1,
        normal2,
        inverse2,
        second,
        upward,
        active,
        result,
    )


def on_device(
    frames, lengths, w_query, w_key, w_value, w_out, w_up, w_down, gain_attn, gain_mlp, cotangent
):
    item_count, slot_len, model_width = frames.shape
    key_mask = lax.broadcasted_iota(jnp.int32, (item_count, slot_len), 1) < lengths[:, None]
    row_mask = key_mask.reshape(item_count * slot_len, 1).astype(jnp.float32)
    gathered = fetch_weights(w_query, w_key, w_value, w_out, w_up, w_down, gain_attn, gain_mlp)
    forward_state = recompute(frames, key_mask, row_mask, gathered)
    output = forward_state[13].astype(jnp.bfloat16).reshape(frames.shape)
    back_weights = fetch_weights(w_query, w_key, w_value, w_out, w_up, w_down, gain_attn, gain_mlp)
    query_mat, key_mat, value_mat, out_mat, up_mat, down_mat, attn_gain, mlp_gain = back_weights
    state = recompute(frames, key_mask, row_mask, back_weights)
    (
        hidden,
        queries,
        key_rows,
        values,
        log_total,
        mixed_low,
        normal1,
        inverse1,
        normal2,
        inverse2,
        second,
        upward,
        active,
        ignored,
    ) = state
    grad_res = cotangent.reshape(item_count * slot_len, model_width).astype(jnp.float32) * row_mask
    grad_branch = grad_res.astype(jnp.bfloat16)
    grad_down = jnp.einsum("rf,rd->fd", active, grad_branch, preferred_element_type=jnp.float32)
    grad_active = jnp.einsum("rd,fd->rf", grad_branch, down_mat, preferred_element_type=jnp.float32)
    unused, gelu_pull = jax.vjp(partial(jax.nn.gelu, approximate=True), upward)
    grad_upward = gelu_pull(grad_active)[0].astype(jnp.bfloat16)
    grad_up = jnp.einsum("rd,rf->df", second, grad_upward, preferred_element_type=jnp.float32)
    grad_second = jnp.einsum("rf,df->rd", grad_upward, up_mat, preferred_element_type=jnp.float32)
    grad_norm2, grad_gain2 = norm_backward(
        grad_second, mlp_gain.astype(jnp.float32), normal2, inverse2
    )
    grad_middle = grad_res + grad_norm2
    grad_attn = grad_middle.astype(jnp.bfloat16)
    grad_outmat = jnp.einsum("rd,re->de", mixed_low, grad_attn, preferred_element_type=jnp.float32)
    grad_mixed = jnp.einsum(
        "re,de->rd", grad_attn, out_mat, preferred_element_type=jnp.float32
    ).astype(jnp.bfloat16)
    grad_mixed = grad_mixed.reshape(item_count, slot_len, HEADS, HEAD_DIM)
    grad_queries, grad_keys, grad_values = lax.map(
        attend_back, (queries, key_rows, values, key_mask, log_total, grad_mixed)
    )
    flat_rows = (item_count * slot_len, model_width)
    grad_queries = grad_queries.reshape(flat_rows)
    grad_keys = grad_keys.reshape(flat_rows)
    grad_values = grad_values.reshape(flat_rows)
    grad_query = jnp.einsum("rd,re->de", hidden, grad_queries, preferred_element_type=jnp.float32)
    grad_key = jnp.einsum("rd,re->de", hidden, grad_keys, preferred_element_type=jnp.float32)
    grad_value = jnp.einsum("rd,re->de", hidden, grad_values, preferred_element_type=jnp.float32)
    grad_hidden = jnp.einsum(
        "re,de->rd", grad_queries, query_mat, preferred_element_type=jnp.float32
    )
    grad_hidden = grad_hidden + jnp.einsum(
        "re,de->rd", grad_keys, key_mat, preferred_element_type=jnp.float32
    )
    grad_hidden = grad_hidden + jnp.einsum(
        "re,de->rd", grad_values, value_mat, preferred_element_type=jnp.float32
    )
    grad_norm1, grad_gain1 = norm_backward(
        grad_hidden, attn_gain.astype(jnp.float32), normal1, inverse1
    )
    grad_frames = (grad_middle + grad_norm1).reshape(frames.shape)
    owned = spread_grads(
        grad_query, grad_key, grad_value, grad_outmat, grad_up, grad_down, grad_gain1, grad_gain2
    )
    return (
        output,
        grad_frames,
        owned[0],
        owned[1],
        owned[2],
        owned[3],
        owned[4],
        owned[5],
        owned[6],
        owned[7],
    )


def solution(mesh):
    return jax.shard_map(
        on_device,
        mesh=mesh,
        in_specs=(
            P(("wide", "narrow"), None, None),
            P(("wide", "narrow")),
            P(("wide", "narrow"), None),
            P(("wide", "narrow"), None),
            P(("wide", "narrow"), None),
            P(("wide", "narrow"), None),
            P(("wide", "narrow"), None),
            P(("wide", "narrow"), None),
            P(("wide", "narrow")),
            P(("wide", "narrow")),
            P(("wide", "narrow"), None, None),
        ),
        out_specs=(
            P(("wide", "narrow"), None, None),
            P(("wide", "narrow"), None, None),
            P(("wide", "narrow"), None),
            P(("wide", "narrow"), None),
            P(("wide", "narrow"), None),
            P(("wide", "narrow"), None),
            P(("wide", "narrow"), None),
            P(("wide", "narrow"), None),
            P(("wide", "narrow")),
            P(("wide", "narrow")),
        ),
        check_vma=False,
    )
```

profile of v0, /device:TPU:0, one launch (start us, length us, event | category | flops | bytes accessed | tf_op | source)
XLA Modules:
  0.0 1361.5 jit_solution(15978379861439638952)
XLA Ops:
  13.5 42.0 %all-reduce.5 = (bf16[1024]{0:T(1024)(128)(2,1)S(1)}, bf16[1024]{0:T(1024)(128)(2,1)S(1)}) all-reduce(bf16[1024]{0:T(1024)(128)(2,1)S(1)} %dynamic-update-slice, bf16[1024]{0:T(1024)(128)(2,1)S(1)} %dynamic-update-slice.1), channel_id=1, replica_groups=mesh['wide'=8,'narrow'=4] {'wide','narrow'}, use_global_device_ids=true, to_apply=%add | all-reduce | flops 2048 | bytes 8192
  55.6 1.5 fusion.27
  57.1 13.0 all-gather.9.cloned.1.call-done
  70.1 3.2 convolution_convert_fusion.2
  73.9 54.3 %all-gather.11.cloned.1.call-done = bf16[1024,1024]{1,0:T(8,128)(2,1)} async-done(((bf16[32,1024]{1,0:T(8,128)(2,1)}), bf16[1024,1024]{1,0:T(8,128)(2,1)}) %all-gather.11.cloned.1.call-update) | async-done | bytes 2097168 | tf_op jit(solution)/shard_map/all_gather | solution.py:30
  128.2 3.9 convolution_convert_fusion.1
  132.1 1.5 copy.43
  133.6 52.8 %all-gather.7.cloned.1.call-done = bf16[1024,1024]{1,0:T(8,128)(2,1)} async-done(((bf16[32,1024]{1,0:T(8,128)(2,1)}), bf16[1024,1024]{1,0:T(8,128)(2,1)}) %all-gather.7.cloned.1.call-update) | async-done | bytes 2097168 | tf_op jit(solution)/shard_map/all_gather | solution.py:31
  186.3 3.9 convolution_convert_fusion.3
  190.2 2.3 copy.41
  192.5 7.6 fusion.59
  200.1 8.4 fusion
  208.4 8.5 fusion.32
  217.0 27.4 %all-gather.13.cloned.1.call-done = bf16[1024,1024]{1,0:T(8,128)(2,1)} async-done(((bf16[32,1024]{1,0:T(8,128)(2,1)}), bf16[1024,1024]{1,0:T(8,128)(2,1)}) %all-gather.13.cloned.1.call-update) | async-done | bytes 2097168 | tf_op jit(solution)/shard_map/all_gather | solution.py:32
  244.3 3.3 multiply_reduce_fusion.3
  247.6 75.7 %all-gather.15.cloned.1.call-done = bf16[1024,4096]{1,0:T(8,128)(2,1)} async-done(((bf16[32,4096]{1,0:T(8,128)(2,1)}), bf16[1024,4096]{1,0:T(8,128)(2,1)}) %all-gather.15.cloned.1.call-update) | async-done | bytes 8388624 | tf_op jit(solution)/shard_map/all_gather | solution.py:33
  323.4 10.4 fusion.49
  333.7 68.4 %all-gather.17.cloned.1.call-done = bf16[4096,1024]{1,0:T(8,128)(2,1)} async-done(((bf16[128,1024]{1,0:T(8,128)(2,1)}), bf16[4096,1024]{1,0:T(8,128)(2,1)}) %all-gather.17.cloned.1.call-update) | async-done | bytes 8388624 | tf_op jit(solution)/shard_map/all_gather | solution.py:34
  402.2 12.9 fusion.8
  415.1 5.4 multiply_reduce_fusion.1
  420.5 2.3 fusion.30
  422.9 3.3 fusion.38
  426.5 3.9 convolution_convert_fusion
  430.4 1.5 copy.45
  431.9 8.8 fusion.33
  441.7 3.5 fusion.50
  445.3 10.6 multiply_reduce_fusion
  455.9 8.1 multiply_convert_fusion
  464.0 1.5 multiply_convert_fusion.3
  465.5 1.8 copy-done
  468.3 3.4 fusion.54
  472.9 6.1 multiply_convert_fusion.2
  480.0 3.4 fusion.52
  484.7 15.1 %fusion.41 = f32[4096,1024]{1,0:T(8,128)} fusion(bf16[1,512,1024]{2,1,0:T(8,128)(2,1)S(1)} %copy-done.20, f32[512]{0:T(512)S(1)} %copy-done.25, f32[512,4096]{1,0:T(8,128)} %fusion.49), kind=kOutput, calls=%fused_computation.62 | convolution fusion | flops 4315414528 | bytes 26216448 | tf_op jit(solution)/shard_map/rf,rd->fd/dot_general | solution.py:179
  500.0 1.3 copy-done.10
  501.4 10.4 fusion.48
  511.8 1.2 copy-done.22
  513.0 3.0 fusion.61
  516.1 1.3 fusion.60
  518.0 3.1 fusion.26
  521.1 39.9 %all-reduce.4 = (f32[1024]{0:T(1024)S(1)}, f32[1024]{0:T(1024)S(1)}) all-reduce(f32[1024]{0:T(1024)S(1)} %get-tuple-element.61, f32[1024]{0:T(1024)S(1)} %copy-done.28), channel_id=8, replica_groups=mesh['wide'=8,'narrow'=4] {'wide','narrow'}, use_global_device_ids=true, to_apply=%region_14.15.clone | all-reduce | flops 2048 | bytes 16384
  562.2 3.6 fusion.25
  565.8 12.0 fusion.36
  577.8 128.3 %reduce-scatter.11.cloned.1.call-done = f32[32,1024]{1,0:T(8,128)} async-done(((f32[1024,1024]{1,0:T(8,128)}), f32[32,1024]{1,0:T(8,128)}) %reduce-scatter.11.cloned.1.call-update) | async-done | bytes 131088 | tf_op jit(solution)/shard_map/reduce_scatter | solution.py:46
  706.1 139.8 %reduce-scatter.7.cloned.1.call-done = f32[32,1024]{1,0:T(8,128)} async-done(((f32[1024,1024]{1,0:T(8,128)}), f32[32,1024]{1,0:T(8,128)}) %reduce-scatter.7.cloned.1.call-update) | async-done | bytes 131088 | tf_op jit(solution)/shard_map/reduce_scatter | solution.py:44
  845.9 139.6 %reduce-scatter.9.cloned.1.call-done = f32[32,1024]{1,0:T(8,128)} async-done(((f32[1024,1024]{1,0:T(8,128)}), f32[32,1024]{1,0:T(8,128)}) %reduce-scatter.9.cloned.1.call-update) | async-done | bytes 131088 | tf_op jit(solution)/shard_map/reduce_scatter | solution.py:45
  985.5 181.6 %reduce-scatter.17.cloned.1.call-done = f32[128,1024]{1,0:T(8,128)} async-done(((f32[4096,1024]{1,0:T(8,128)}), f32[128,1024]{1,0:T(8,128)}) %reduce-scatter.17.cloned.1.call-update) | async-done | bytes 524304 | tf_op jit(solution)/shard_map/reduce_scatter | solution.py:49
  1167.0 187.4 %reduce-scatter.15.cloned.1.call-done = f32[32,4096]{1,0:T(8,128)} async-done(((f32[1024,4096]{1,0:T(8,128)}), f32[32,4096]{1,0:T(8,128)}) %reduce-scatter.15.cloned.1.call-update) | async-done | bytes 524304 | tf_op jit(solution)/shard_map/reduce_scatter | solution.py:48
  (102 shorter events, 14.1 us)
Async XLA Ops:
  7.2 62.9 %all-gather.9.cloned.1.call-start = ((), (), s32[]{:S(2)}) async-start(), calls=%async_computation.7 | async-start | bytes 2162688 | tf_op jit(solution)/shard_map/all_gather | solution.py:29
  7.9 120.3 %all-gather.11.cloned.1.call-start = ((), (), s32[]{:S(2)}) async-start(), calls=%async_computation.8 | async-start | bytes 2162688 | tf_op jit(solution)/shard_map/all_gather | solution.py:30
  8.7 177.7 %all-gather.7.cloned.1.call-start = ((), (), s32[]{:S(2)}) async-start(), calls=%async_computation.6 | async-start | bytes 2162688 | tf_op jit(solution)/shard_map/all_gather | solution.py:31
  9.4 234.9 %all-gather.13.cloned.1.call-start = ((), (), s32[]{:S(2)}) async-start(), calls=%async_computation.9 | async-start | bytes 2162688 | tf_op jit(solution)/shard_map/all_gather | solution.py:32
  10.0 313.4 %all-gather.15.cloned.1.call-start = ((), (), s32[]{:S(2)}) async-start(), calls=%async_computation.10 | async-start | bytes 8650752 | tf_op jit(solution)/shard_map/all_gather | solution.py:33
  10.6 391.6 %all-gather.17.cloned.1.call-start = ((), (), s32[]{:S(2)}) async-start(), calls=%async_computation.11 | async-start | bytes 8650752 | tf_op jit(solution)/shard_map/all_gather | solution.py:34
  11.1 566.7 %reduce-scatter.13.cloned.1.call-start = ((), (), s32[]{:S(2)}) async-start(), calls=%async_computation.15 | async-start | bytes 4325376 | tf_op jit(solution)/shard_map/reduce_scatter | solution.py:47
  55.6 364.9 %copy-start.24 = (f32[512]{0:T(512)}, f32[512]{0:T(512)S(1)}, u32[]{:S(2)}) copy-start(f32[512]{0:T(512)S(1)} %fusion.47) | copy-start | bytes 6148
  57.1 71.1 %copy-start.3 = (bf16[1,512,1024]{2,1,0:T(8,128)(2,1)S(1)}, bf16[1,512,1024]{2,1,0:T(8,128)(2,1)}, u32[]{:S(2)}) copy-start(bf16[1,512,1024]{2,1,0:T(8,128)(2,1)} %param.11) | copy-start | bytes 3145732
  73.9 118.6 %copy-start.7 = (bf16[512,1024]{0,1:T(8,128)(2,1)}, bf16[512,1024]{0,1:T(8,128)(2,1)S(1)}, u32[]{:S(2)}) copy-start(bf16[512,1024]{0,1:T(8,128)(2,1)S(1)} %copy.42) | copy-start | bytes 3145732
  133.6 58.9 %copy-start.4 = (bf16[512,1024]{0,1:T(8,128)(2,1)}, bf16[512,1024]{0,1:T(8,128)(2,1)S(1)}, u32[]{:S(2)}) copy-start(bf16[512,1024]{0,1:T(8,128)(2,1)S(1)} %copy.43) | copy-start | bytes 3145732
  200.1 8.4 copy-start.13
  247.6 167.5 %copy-start.9 = (f32[512,1024]{1,0:T(8,128)}, f32[512,1024]{1,0:T(8,128)S(1)}, u32[]{:S(2)}) copy-start(f32[512,1024]{1,0:T(8,128)S(1)} %get-tuple-element.80) | copy-start | bytes 6291460
  247.6 172.9 %copy-start.26 = (f32[512]{0:T(512)}, f32[512]{0:T(512)S(1)}, u32[]{:S(2)}) copy-start(f32[512]{0:T(512)S(1)} %add_rsqrt_fusion) | copy-start | bytes 6148
  402.1 12.9 copy-start.29
  415.1 5.4 copy-start.31
  415.1 5.4 copy-start.19
  420.5 2.4 copy-start.12
  422.8 3.7 copy-start.1
  426.2 279.9 %reduce-scatter.11.cloned.1.call-start = ((), (), s32[]{:S(2)}) async-start(), calls=%async_computation.14 | async-start | bytes 4325376 | tf_op jit(solution)/shard_map/reduce_scatter | solution.py:46
  426.5 5.4 copy-start.23
  431.9 8.8 copy-start.6
  440.7 1.0 copy-start.14
  445.2 400.7 %reduce-scatter.7.cloned.1.call-start = ((), (), s32[]{:S(2)}) async-start(), calls=%async_computation.12 | async-start | bytes 4325376 | tf_op jit(solution)/shard_map/reduce_scatter | solution.py:44
  455.9 8.1 copy-start.5
  464.0 3.2 copy-start
  467.2 1.0 copy-start.16
  471.7 1.2 copy-start.8
  471.7 513.7 %reduce-scatter.9.cloned.1.call-start = ((), (), s32[]{:S(2)}) async-start(), calls=%async_computation.13 | async-start | bytes 4325376 | tf_op jit(solution)/shard_map/reduce_scatter | solution.py:45
  479.0 1.0 copy-start.21
  483.4 1.2 copy-start.20
  483.4 1.2 copy-start.25
  483.5 683.6 %reduce-scatter.17.cloned.1.call-start = ((), (), s32[]{:S(2)}) async-start(), calls=%async_computation.17 | async-start | bytes 17301504 | tf_op jit(solution)/shard_map/reduce_scatter | solution.py:49
  499.8 1.6 copy-start.10
  499.8 1.6 copy-start.27
  499.8 854.6 %reduce-scatter.15.cloned.1.call-start = ((), (), s32[]{:S(2)}) async-start(), calls=%async_computation.16 | async-start | bytes 17301504 | tf_op jit(solution)/shard_map/reduce_scatter | solution.py:48
  511.8 1.2 copy-start.22
  513.0 3.1 copy-start.17
  513.0 3.1 copy-start.30
  516.1 1.3 copy-start.15
  516.1 1.9 copy-start.18
  518.0 3.1 copy-start.28
  518.0 44.2 %copy-start.2 = (f32[512,1024]{1,0:T(8,128)S(1)}, f32[512,1024]{1,0:T(8,128)}, u32[]{:S(2)}) copy-start(f32[512,1024]{1,0:T(8,128)} %copy-done.1) | copy-start | bytes 6291460
  562.2 3.6 copy-start.11
Sparse Core Ops, SparseCore 0:
  10.9 59.1 all-gather.8
  73.0 55.2 all-gather.10
  131.1 55.2 all-gather.6
  189.0 55.2 all-gather.12
  247.0 76.2 all-gather.14
  326.1 76.0 all-gather.16
  426.3 139.8 reduce-scatter.12
  569.1 136.9 reduce-scatter.10
  709.0 136.9 reduce-scatter.6
  848.6 136.8 reduce-scatter.8
  988.3 178.6 reduce-scatter.16
  1169.8 184.6 reduce-scatter.14
where the time goes:
time: 1370 us; the launch traced here: 1360 us
  waiting for transfers between devices  1070 us (78%)
  matrix products  148 us (11%)
  blocking collectives  81.9 us (6%)
  other arithmetic  23.9 us (2%)
  local copies, waits for them, and re-layouts  18.6 us (1%)
  between operations  15.5 us (1%)
    reduce_scatter x1, waiting for transfers between devices, spread_grads(): lax.psum_scatter(grad_up, ('wide', 'narrow'), scatter_dimension=0, tiled=...  187 us
    reduce_scatter x1, waiting for transfers between devices, spread_grads(): lax.psum_scatter(grad_down, ('wide', 'narrow'), scatter_dimension=0, tile...  182 us
    reduce_scatter x1, waiting for transfers between devices, spread_grads(): lax.psum_scatter(grad_query, ('wide', 'narrow'), scatter_dimension=0, til...  140 us
    reduce_scatter x1, waiting for transfers between devices, spread_grads(): lax.psum_scatter(grad_key, ('wide', 'narrow'), scatter_dimension=0, tiled...  140 us
    reduce_scatter x1, waiting for transfers between devices, spread_grads(): lax.psum_scatter(grad_value, ('wide', 'narrow'), scatter_dimension=0, til...  128 us
    unnamed x2, blocking collectives  81.9 us
    all_gather x1, waiting for transfers between devices, fetch_weights(): lax.all_gather(w_up, ('wide', 'narrow'), axis=0, tiled=True)  75.7 us
    all_gather x1, waiting for transfers between devices, fetch_weights(): lax.all_gather(w_down, ('wide', 'narrow'), axis=0, tiled=True)  68.4 us
  transfers between devices with their start and end apart: 12, of which 11 were waited for; matrix products, arithmetic and copies ran while one was open for 12% of the time, Pallas kernels for 0%

commit v1 on v0

--- a/solution.py
+++ b/solution.py
@@ -24,31 +24,64 @@
     return (grad_rows, jnp.sum(grad_in * normal, axis=0))
 
 
+AXES = ("wide", "narrow")
+LANES = 128
+
+
+def gather_rows(shard):
+    return lax.all_gather(shard, AXES, axis=0, tiled=True)
+
+
+def scatter_rows(grad):
+    return lax.psum_scatter(grad.astype(jnp.bfloat16), AXES, scatter_dimension=0, tiled=True).astype(jnp.float32)
+
+
 def fetch_weights(w_query, w_key, w_value, w_out, w_up, w_down, gain_attn, gain_mlp):
-    return (
-        lax.all_gather(w_query, ("wide", "narrow"), axis=0, tiled=True),
-        lax.all_gather(w_key, ("wide", "narrow"), axis=0, tiled=True),
-        lax.all_gather(w_value, ("wide", "narrow"), axis=0, tiled=True),
-        lax.all_gather(w_out, ("wide", "narrow"), axis=0, tiled=True),
-        lax.all_gather(w_up, ("wide", "narrow"), axis=0, tiled=True),
-        lax.all_gather(w_down, ("wide", "narrow"), axis=0, tiled=True),
-        lax.all_gather(gain_attn, ("wide", "narrow"), axis=0, tiled=True),
-        lax.all_gather(gain_mlp, ("wide", "narrow"), axis=0, tiled=True),
-    )
+    width = w_query.shape[1]
+    gains = jnp.stack((gain_attn, gain_mlp), axis=1)
+    gains = jnp.pad(gains, ((0, 0), (0, LANES - 2)))
+    attn = gather_rows(jnp.concatenate((w_query, w_key, w_value, w_out, gains), axis=1))
+    up_mat = gather_rows(w_up)
+    down_mat = gather_rows(w_down)
+    gain_pair = attn[:, 4 * width : 4 * width + 2].T
+    return (
+        attn[:, :width],
+        attn[:, width : 2 * width],
+        attn[:, 2 * width : 3 * width],
+        attn[:, 3 * width : 4 * width],
+        up_mat,
+        down_mat,
+        gain_pair[0],
+        gain_pair[1],
+    )
+
+
+def split_halves(values):
+    high = values.astype(jnp.bfloat16)
+    low = (values - high.astype(jnp.float32)).astype(jnp.bfloat16)
+    return (high, low)
 
 
 def spread_grads(
     grad_query, grad_key, grad_value, grad_outmat, grad_up, grad_down, grad_gain1, grad_gain2
 ):
-    return (
-        lax.psum_scatter(grad_query, ("wide", "narrow"), scatter_dimension=0, tiled=True),
-        lax.psum_scatter(grad_key, ("wide", "narrow"), scatter_dimension=0, tiled=True),
-        lax.psum_scatter(grad_value, ("wide", "narrow"), scatter_dimension=0, tiled=True),
-        lax.psum_scatter(grad_outmat, ("wide", "narrow"), scatter_dimension=0, tiled=True),
-        lax.psum_scatter(grad_up, ("wide", "narrow"), scatter_dimension=0, tiled=True),
-        lax.psum_scatter(grad_down, ("wide", "narrow"), scatter_dimension=0, tiled=True),
-        lax.psum_scatter(grad_gain1, ("wide", "narrow"), scatter_dimension=0, tiled=True),
-        lax.psum_scatter(grad_gain2, ("wide", "narrow"), scatter_dimension=0, tiled=True),
+    width = grad_query.shape[1]
+    down_rows = scatter_rows(grad_down)
+    up_rows = scatter_rows(grad_up)
+    gains = jnp.stack(split_halves(grad_gain1) + split_halves(grad_gain2), axis=1)
+    gains = jnp.pad(gains, ((0, 0), (0, LANES - 4)))
+    joined = [part.astype(jnp.bfloat16) for part in (grad_query, grad_key, grad_value, grad_outmat)]
+    rows = scatter_rows(jnp.concatenate(joined + [gains], axis=1))
+    extra = rows[:, 4 * width :]
+    return (
+        rows[:, :width],
+        rows[:, width : 2 * width],
+        rows[:, 2 * width : 3 * width],
+        rows[:, 3 * width : 4 * width],
+        up_rows,
+        down_rows,
+        extra[:, 0] + extra[:, 1],
+        extra[:, 2] + extra[:, 3],
     )
 
 
@@ -155,9 +188,8 @@
     gathered = fetch_weights(w_query, w_key, w_value, w_out, w_up, w_down, gain_attn, gain_mlp)
     forward_state = recompute(frames, key_mask, row_mask, gathered)
     output = forward_state[13].astype(jnp.bfloat16).reshape(frames.shape)
-    back_weights = fetch_weights(w_query, w_key, w_value, w_out, w_up, w_down, gain_attn, gain_mlp)
-    query_mat, key_mat, value_mat, out_mat, up_mat, down_mat, attn_gain, mlp_gain = back_weights
-    state = recompute(frames, key_mask, row_mask, back_weights)
+    query_mat, key_mat, value_mat, out_mat, up_mat, down_mat, attn_gain, mlp_gain = gathered
+    state = forward_state
     (
         hidden,
         queries,

time: 1370 us -> 796 us (0.58)
  waiting for transfers between devices: 1070 us -> 558 us
  blocking collectives: 81.9 us -> 0 us
  local copies, waits for them, and re-layouts: 18.6 us -> 35.4 us
    reduce_scatter x6 -> x2, waiting for transfers between devices: 777 us -> 284 us  [scatter_rows(): lax.psum_scatter(grad.astype(jnp.bfloat16), AXES, scatter_dimension=0, ti...]
    all_gather x6 -> x3, waiting for transfers between devices: 292 us -> 181 us  [gather_rows(): return lax.all_gather(shard, AXES, axis=0, tiled=True)]
    unnamed x12 -> x7, waiting for transfers between devices: 3.73 us -> 92.3 us
    unnamed x2 -> x0, blocking collectives: 81.9 us -> none
    unnamed x70 -> x77, local copies, waits for them, and re-layouts: 12.8 us -> 28.1 us
  transfers between devices with their start and end apart: 12 -> 6, of which waited for: 11 -> 6; matrix products, arithmetic and copies ran while one was open for 12% -> 14% of each run, Pallas kernels for 0% -> 0%
where the time goes in v1:
time: 796 us; the launch traced here: 785 us
  waiting for transfers between devices  558 us (70%)
  matrix products  145 us (18%)
  local copies, waits for them, and re-layouts  35.4 us (4%)
  other arithmetic  31.6 us (4%)
  between operations  15.6 us (2%)
    reduce_scatter x2, waiting for transfers between devices, scatter_rows(): lax.psum_scatter(grad.astype(jnp.bfloat16), AXES, scatter_dimension=0, ti...  284 us
    all_gather x3, waiting for transfers between devices, gather_rows(): return lax.all_gather(shard, AXES, axis=0, tiled=True)  181 us
    unnamed x7, waiting for transfers between devices  92.3 us
    unnamed x77, local copies, waits for them, and re-layouts  28.1 us
  transfers between devices with their start and end apart: 6, of which 6 were waited for; matrix products, arithmetic and copies ran while one was open for 14% of the time, Pallas kernels for 0%

profile of v1, /device:TPU:0, one launch (start us, length us, event | category | flops | bytes accessed | tf_op | source)
XLA Modules:
  0.0 785.5 jit_solution(17129673790001334419)
XLA Ops:
  14.8 1.5 fusion.27
  16.4 77.1 %all-gather.4.cloned.1.call-done = bf16[1024,4224]{1,0:T(8,128)(2,1)} async-done(((bf16[32,4224]{1,0:T(8,128)(2,1)}), bf16[1024,4224]{1,0:T(8,128)(2,1)}) %all-gather.4.cloned.1.call-update) | async-done | bytes 8650768 | tf_op jit(solution)/shard_map/all_gather | solution.py:32
  93.4 1.0 slice_bitcast_fusion
  94.7 3.3 fusion.54
  98.6 4.2 fusion.57
  102.9 1.5 copy.54
  104.4 3.9 fusion.51
  108.3 1.5 copy.52
  109.8 7.6 fusion.96
  117.4 8.5 %fusion = f32[16,512]{1,0:T(8,128)S(1)} fusion(f32[16,512,512]{1,2,0:T(8,128)} %get-tuple-element.104, f32[16,512]{1,0:T(8,128)S(1)} %get-tuple-element.103), kind=kLoop, calls=%fused_computation.6 | loop fusion | flops 8380416 | bytes 16842752 | tf_op jit(solution)/shard_map/while/body/eval_jaxpr/reduce_sum | solution.py:101
  125.9 7.6 fusion.50
  133.6 3.3 multiply_reduce_fusion.3
  137.0 35.4 %all-gather.6.cloned.1.call-done = bf16[1024,4096]{1,0:T(8,128)(2,1)} async-done(((bf16[32,4096]{1,0:T(8,128)(2,1)}), bf16[1024,4096]{1,0:T(8,128)(2,1)}) %all-gather.6.cloned.1.call-update) | async-done | bytes 8388624 | tf_op jit(solution)/shard_map/all_gather | solution.py:32
  172.4 10.3 %fusion.88 = f32[512,4096]{1,0:T(8,128)} fusion(bf16[1024,4096]{1,0:T(8,128)(2,1)} %all-gather.6.cloned.1.call-done, f32[512,1024]{1,0:T(8,128)S(1)} %get-tuple-element.106, f32[1024]{0:T(1024)S(1)} %get-tuple-element.95, f32[512]{0:T(512)S(1)} %add_rsqrt_fusion), kind=kOutput, calls=%fused_computation.115 | convolution fusion | flops 4296540160 | bytes 18880512 | tf_op jit(solution)/shard_map/dot_general | solution.py:161
  182.7 68.7 %all-gather.8.cloned.1.call-done = bf16[4096,1024]{1,0:T(8,128)(2,1)} async-done(((bf16[128,1024]{1,0:T(8,128)(2,1)}), bf16[4096,1024]{1,0:T(8,128)(2,1)}) %all-gather.8.cloned.1.call-update) | async-done | bytes 8388624 | tf_op jit(solution)/shard_map/all_gather | solution.py:32
  251.4 13.2 %fusion.8 = bf16[512,4096]{1,0:T(8,128)(2,1)S(1)} fusion(f32[512,4096]{1,0:T(8,128)} %fusion.88, bf16[4096,1024]{1,0:T(8,128)(2,1)} %all-gather.8.cloned.1.call-done, bf16[1,512,1024]{2,1,0:T(8,128)(2,1)} %param.21, f32[512]{0:T(512)S(1)} %fusion.87), kind=kOutput, calls=%fused_computation.16 | convolution fusion | flops 4338483200 | bytes 22022144 | tf_op jit(solution)/shard_map/rd,fd->rf/dot_general | solution.py:212
  264.7 4.8 multiply_reduce_fusion.1
  270.3 1.3 copy-done.2
  271.6 2.9 fusion.60
  274.5 1.3 copy.56
  275.8 9.9 %fusion.63 = bf16[16,64,512]{2,1,0:T(8,128)(2,1)} fusion(bf16[512,16,64]{0,2,1:T(8,128)(2,1)} %bitcast.12, f32[16,512,512]{1,2,0:T(8,128)} %get-tuple-element.104, f32[16,512]{1,0:T(8,128)S(1)} %log_add_fusion), kind=kOutput, calls=%fused_computation.78 | convolution fusion | flops 545783808 | bytes 18907136 | tf_op jit(solution)/shard_map/while/body/eval_jaxpr/hqk,qhd->khd/dot_general | solution.py:112
  285.8 14.6 %multiply_reduce_fusion = (f32[16,512]{1,0:T(8,128)}, f32[16,512,512]{1,2,0:T(8,128)}) fusion(f32[16,512,512]{1,2,0:T(8,128)} %get-tuple-element.104, f32[16,512]{1,0:T(8,128)} %copy-done.12, bf16[512,16,64]{0,2,1:T(8,128)(2,1)} %bitcast.12, bf16[512,16,64]{0,2,1:T(8,128)(2,1)} %bitcast.113), kind=kOutput, calls=%fused_computation.1 | convolution fusion | flops 549445632 | bytes 35717120 | tf_op jit(solution)/shard_map/while/body/eval_jaxpr/qhd,khd->hqk/dot_general | solution.py:115
  300.4 10.7 %multiply_convert_fusion = bf16[16,512,512]{1,2,0:T(8,128)(2,1)} fusion(f32[16,512,512]{1,2,0:T(8,128)} %get-tuple-element.109, f32[16,512,512]{1,2,0:T(8,128)S(1)} %bitcast.107, f32[16,512]{1,0:T(8,128)} %get-tuple-element.108, f32[16,512]{1,0:T(8,128)} %copy-done.12), kind=kLoop, calls=%fused_computation | loop fusion | flops 16777216 | bytes 42008576 | tf_op jit(solution)/shard_map/while/body/eval_jaxpr/convert_element_type | solution.py:118
  311.1 6.5 multiply_convert_fusion.2
  317.6 1.5 multiply_convert_fusion.3
  319.8 1.3 fusion.36
  321.1 1.3 fusion.40
  322.6 3.2 fusion.26
  325.8 2.7 convert_dynamic-update-slice_fusion.3
  328.5 2.7 convert_dynamic-update-slice_fusion.2
  331.3 2.7 convert_dynamic-update-slice_fusion.1
  334.0 2.6 convert_dynamic-update-slice_fusion
  337.4 11.5 %copy.68 = bf16[1024,4224]{1,0:T(8,128)(2,1)} copy(bf16[1024,4224]{0,1:T(8,128)(2,1)} %fusion.84) | data formatting | bytes 17301504
  349.5 10.9 %convolution_convert_fusion = bf16[4096,1024]{1,0:T(8,128)(2,1)} fusion(bf16[1,512,1024]{2,1,0:T(8,128)(2,1)} %param.21, f32[512]{0:T(512)S(1)} %copy-done.16, f32[512,4096]{1,0:T(8,128)} %fusion.88), kind=kOutput, calls=%fused_computation.21 | convolution fusion | flops 4319608832 | bytes 17827840 | tf_op jit(solution)/shard_map/rf,rd->fd/dot_general | solution.py:211
  361.1 11.0 %convolution_convert_fusion.1 = bf16[1024,4096]{1,0:T(8,128)(2,1)} fusion(bf16[512,4096]{1,0:T(8,128)(2,1)} %copy-done.25, f32[512,1024]{1,0:T(8,128)} %copy-done.8, f32[1024]{0:T(1024)S(1)} %get-tuple-element.95, f32[512]{0:T(512)S(1)} %copy-done.20), kind=kOutput, calls=%fused_computation.22 | convolution fusion | flops 4300734464 | bytes 14686208 | tf_op jit(solution)/shard_map/rd,rf->df/dot_general | solution.py:215
  372.2 3.7 fusion.25
  375.9 12.6 %fusion.68 = bf16[1,512,1024]{2,1,0:T(8,128)(2,1)} fusion(f32[512,1024]{1,0:T(8,128)S(1)} %copy-done.9, bf16[4096,1024]{1,0:T(8,128)(2,1)} %all-gather.8.cloned.1.call-done, f32[512]{0:T(512)S(1)} %copy-done.16, f32[512,4096]{1,0:T(8,128)} %fusion.88), kind=kOutput, calls=%fused_computation.79 | convolution fusion | flops 4315414528 | bytes 19924992 | tf_op jit(solution)/shard_map/dot_general | solution.py:163
  388.5 90.9 %reduce-scatter.10.cloned.1.call-done = bf16[32,4224]{1,0:T(8,128)(2,1)} async-done(((bf16[1024,4224]{1,0:T(8,128)(2,1)}), bf16[32,4224]{1,0:T(8,128)(2,1)}) %reduce-scatter.10.cloned.1.call-update) | async-done | bytes 270352
  479.4 1.5 copy.69
  481.0 1.4 fusion.95
  482.4 1.9 copy.63
  484.2 1.9 copy.62
  486.1 1.9 copy.61
  488.0 1.9 copy.60
  490.4 139.1 %reduce-scatter.8.cloned.1.call-done = bf16[128,1024]{1,0:T(8,128)(2,1)} async-done(((bf16[4096,1024]{1,0:T(8,128)(2,1)}), bf16[128,1024]{1,0:T(8,128)(2,1)}) %reduce-scatter.8.cloned.1.call-update) | async-done | bytes 262160 | tf_op jit(solution)/shard_map/reduce_scatter | solution.py:36
  629.5 1.8 convert_element_type.257
  631.3 145.1 %reduce-scatter.6.cloned.1.call-done = bf16[32,4096]{1,0:T(8,128)(2,1)} async-done(((bf16[1024,4096]{1,0:T(8,128)(2,1)}), bf16[32,4096]{1,0:T(8,128)(2,1)}) %reduce-scatter.6.cloned.1.call-update) | async-done | bytes 262160 | tf_op jit(solution)/shard_map/reduce_scatter | solution.py:36
  776.5 1.8 convert_element_type.255
  (102 shorter events, 12.2 us)
Async XLA Ops:
  7.2 86.3 %all-gather.4.cloned.1.call-start = ((), (), s32[]{:S(2)}) async-start(), calls=%async_computation.3 | async-start | bytes 8921088 | tf_op jit(solution)/shard_map/all_gather | solution.py:32
  11.4 0.7 copy-start.13
  12.1 160.3 %all-gather.6.cloned.1.call-start = ((), (), s32[]{:S(2)}) async-start(), calls=%async_computation.4 | async-start | bytes 8650752 | tf_op jit(solution)/shard_map/all_gather | solution.py:32
  12.9 238.5 %all-gather.8.cloned.1.call-start = ((), (), s32[]{:S(2)}) async-start(), calls=%async_computation.5 | async-start | bytes 8650752 | tf_op jit(solution)/shard_map/all_gather | solution.py:32
  13.6 465.8 %reduce-scatter.10.cloned.1.call-start = ((), (), s32[]{:S(2)}) async-start(), calls=%async_computation.8 | async-start | bytes 8921088
  14.8 236.6 %copy-start.14 = (f32[512]{0:T(512)}, f32[512]{0:T(512)S(1)}, u32[]{:S(2)}) copy-start(f32[512]{0:T(512)S(1)} %fusion.87) | copy-start | bytes 6148
  16.3 82.2 %copy-start.17 = (f32[512]{0:T(512)}, f32[512]{0:T(512)S(1)}, u32[]{:S(2)}) copy-start(f32[512]{0:T(512)S(1)} %add_rsqrt_fusion.1) | copy-start | bytes 6148
  94.7 3.9 copy-start.5
  98.6 11.2 %copy-start.1 = (bf16[512,1024]{0,1:T(8,128)(2,1)}, bf16[512,1024]{0,1:T(8,128)(2,1)S(1)}, u32[]{:S(2)}) copy-start(bf16[512,1024]{0,1:T(8,128)(2,1)S(1)} %copy.53) | copy-start | bytes 3145732
  104.4 5.4 copy-start.21
  109.8 16.1 %copy-start.4 = (bf16[512,1024]{0,1:T(8,128)(2,1)}, bf16[512,1024]{0,1:T(8,128)(2,1)S(1)}, u32[]{:S(2)}) copy-start(bf16[512,1024]{0,1:T(8,128)(2,1)S(1)} %copy.52) | copy-start | bytes 3145732
  125.9 7.7 copy-start.6
  133.6 3.4 copy-start.23
  136.9 132.6 %copy-start.8 = (f32[512,1024]{1,0:T(8,128)}, f32[512,1024]{1,0:T(8,128)S(1)}, u32[]{:S(2)}) copy-start(f32[512,1024]{1,0:T(8,128)S(1)} %get-tuple-element.106) | copy-start | bytes 6291460
  136.9 132.6 %copy-start.19 = (f32[512]{0:T(512)}, f32[512]{0:T(512)S(1)}, u32[]{:S(2)}) copy-start(f32[512]{0:T(512)S(1)} %add_rsqrt_fusion) | copy-start | bytes 6148
  137.0 138.9 %copy-start.12 = (f32[16,512]{1,0:T(8,128)}, f32[16,512]{1,0:T(8,128)S(1)}, u32[]{:S(2)}) copy-start(f32[16,512]{1,0:T(8,128)S(1)} %log_add_fusion) | copy-start | bytes 98308
  251.4 13.2 %copy-start.22 = (bf16[1024,4096]{1,0:T(8,128)(2,1)S(1)}, bf16[1024,4096]{1,0:T(8,128)(2,1)}, u32[]{:S(2)}) copy-start(bf16[1024,4096]{1,0:T(8,128)(2,1)} %all-gather.6.cloned.1.call-done) | copy-start | bytes 25165828
  264.6 4.9 copy-start.25
  264.6 4.9 copy-start.10
  264.7 4.9 copy-start.15
  270.3 1.3 copy-start.2
  275.8 24.5 %slice-start = ((s8[16777216]{0:T(1024)(128)(4,1)}), s8[4194304]{0:T(1024)(128)(4,1)S(1)}, s32[]{:S(2)}) async-start(s8[16777216]{0:T(1024)(128)(4,1)} %bitcast.106), calls=%async_computation.9 | async-start | bytes 8388608
  275.8 24.5 %slice-start.1 = ((s8[16777216]{0:T(1024)(128)(4,1)}), s8[4194304]{0:T(1024)(128)(4,1)S(1)}, s32[]{:S(2)}) async-start(s8[16777216]{0:T(1024)(128)(4,1)} %bitcast.106), calls=%async_computation.10 | async-start | bytes 8388608
  285.8 14.6 %slice-start.2 = ((s8[16777216]{0:T(1024)(128)(4,1)}), s8[4194304]{0:T(1024)(128)(4,1)S(1)}, s32[]{:S(2)}) async-start(s8[16777216]{0:T(1024)(128)(4,1)} %bitcast.106), calls=%async_computation.11 | async-start | bytes 8388608
  285.8 14.6 %slice-start.3 = ((s8[16777216]{0:T(1024)(128)(4,1)}), s8[4194304]{0:T(1024)(128)(4,1)S(1)}, s32[]{:S(2)}) async-start(s8[16777216]{0:T(1024)(128)(4,1)} %bitcast.106), calls=%async_computation.12 | async-start | bytes 8388608
  311.1 6.5 copy-start
  311.1 8.0 %slice-start.4 = ((s8[8650752]{0:T(1024)(128)(4,1)}), s8[4194304]{0:T(1024)(128)(4,1)S(1)}, s32[]{:S(2)}) async-start(s8[8650752]{0:T(1024)(128)(4,1)} %bitcast.124), calls=%async_computation.13 | async-start | bytes 8388608
  311.1 8.5 %slice-start.5 = ((s8[8650752]{0:T(1024)(128)(4,1)}), s8[4194304]{0:T(1024)(128)(4,1)S(1)}, s32[]{:S(2)}) async-start(s8[8650752]{0:T(1024)(128)(4,1)} %bitcast.124), calls=%async_computation.14 | async-start | bytes 8388608
  317.6 2.1 slice-start.6
  321.1 1.3 copy-start.7
  321.1 1.5 copy-start.11
  321.1 1.5 copy-start.18
  331.3 2.7 copy-start.3
  331.3 2.7 copy-start.24
  348.9 0.7 copy-start.16
  348.9 280.6 %reduce-scatter.8.cloned.1.call-start = ((), (), s32[]{:S(2)}) async-start(), calls=%async_computation.7 | async-start | bytes 8650752 | tf_op jit(solution)/shard_map/reduce_scatter | solution.py:36
  360.4 0.7 copy-start.20
  360.5 416.0 %reduce-scatter.6.cloned.1.call-start = ((), (), s32[]{:S(2)}) async-start(), calls=%async_computation.6 | async-start | bytes 8650752 | tf_op jit(solution)/shard_map/reduce_scatter | solution.py:36
  372.2 3.7 copy-start.9
Sparse Core Ops, SparseCore 0:
  12.3 81.1 all-gather.3
  96.3 76.0 all-gather.5
  175.3 76.0 all-gather.7
  349.0 130.3 reduce-scatter.9
  481.5 147.9 reduce-scatter.7
  631.7 144.7 reduce-scatter.5

commit v2 on v0

v2 whole, which is shorter than its diff:
```python
import functools

import jax
import jax.numpy as jnp
import numpy as np
from jax import lax
from jax.experimental import pallas as pl
from jax.experimental.pallas import tpu as pltpu
from jax.sharding import Mesh, PartitionSpec as P

HEADS = 16
HEAD_DIM = 64
EPSILON = 1e-06
FACTOR = HEAD_DIM ** (-0.5)
LANES = 128
Z_PARTS = 4
PIECES = 8
ALL = ("z", "y", "x", "c")
PLANE = ("y", "x", "c")
SWAP = [(0, 1), (1, 0)]
VMEM_LIMIT = 56 << 20
F32 = jnp.float32
BF16 = jnp.bfloat16
GELU_A = 0.7978845608028654
GELU_B = 0.044715

NN = (((1,), (0,)), ((), ()))
NT = (((1,), (1,)), ((), ()))
TN = (((0,), (0,)), ((), ()))


def mxu(left, right, dims=NN):
    return lax.dot_general(left, right, dims, preferred_element_type=F32)


def plane_pairs(step):
    pairs = []
    for y in range(2):
        for x in range(2):
            for c in range(2):
                flip_y = (c == 0) == (step == 1)
                to = (1 - y, x, c) if flip_y else (y, 1 - x, c)
                pairs.append(((y * 2 + x) * 2 + c, (to[0] * 2 + to[1]) * 2 + to[2]))
    return pairs


def is_plane(sizes):
    return sizes["x"] == 2 and sizes["y"] == 2 and sizes["c"] == 2 and sizes["z"] == Z_PARTS


def piece_blocks(sizes):
    piece = jnp.arange(PIECES, dtype=jnp.int32)
    if not is_plane(sizes):
        return piece
    own = (piece >> 2) & 1
    first = (piece >> 1) & 1
    second = piece & 1
    core = lax.axis_index("c") ^ own
    on_y = jnp.where(core == 0, first, second)
    on_x = jnp.where(core == 0, second, first)
    y = lax.axis_index("y") ^ on_y
    x = lax.axis_index("x") ^ on_x
    return ((y * 2 + x) * 2 + core).astype(jnp.int32)


def gather_pieces(shard, sizes):
    if not is_plane(sizes):
        full = lax.all_gather(shard, ALL, axis=0, tiled=True)
        full = full.reshape(Z_PARTS, PIECES, full.shape[0] // (Z_PARTS * PIECES), full.shape[1])
        full = full.transpose(1, 0, 2, 3).reshape((2, 2, 2, Z_PARTS) + full.shape[2:])
        return (full[0, :, 0], full[0, :, 1], full[1, :, 0], full[1, :, 1])
    column = lax.all_gather(shard, "z", axis=0, tiled=False)
    near = lax.ppermute(column, PLANE, plane_pairs(1))
    own = jnp.stack((column, near))
    far = lax.ppermute(own, PLANE, plane_pairs(2))
    return (own, far, lax.ppermute(own, "c", SWAP), lax.ppermute(far, "c", SWAP))


def total(*parts):
    result = parts[0].astype(F32)
    for part in parts[1:]:
        result = result + part.astype(F32)
    return result


def scatter_pieces(own, other, sizes):
    if not is_plane(sizes):
        full = jnp.stack((own, other))
        full = full.reshape((PIECES,) + full.shape[3:]).transpose(1, 0, 2, 3)
        full = full.reshape(-1, full.shape[-1])
        return lax.psum_scatter(full, ALL, scatter_dimension=0, tiled=True).astype(F32)
    got = lax.ppermute(other, "c", SWAP)
    away = total(own[1], got[1]).astype(BF16)
    near = lax.ppermute(away, PLANE, plane_pairs(1))
    away = total(own[0, 1], got[0, 1], near[1]).astype(BF16)
    far = lax.ppermute(away, PLANE, plane_pairs(2))
    mine = total(own[0, 0], got[0, 0], near[0], far).astype(BF16)
    return lax.psum_scatter(mine, "z", scatter_dimension=0, tiled=False).astype(F32)


def params(**more):
    return pltpu.CompilerParams(vmem_limit_bytes=VMEM_LIMIT, **more)


HBM_SPEC = pl.BlockSpec(memory_space=pl.ANY)
SMEM_SPEC = pl.BlockSpec(memory_space=pltpu.SMEM)


def whole(shape):
    return pl.BlockSpec(shape, lambda *_: (0,) * len(shape))


def piece_copies(pieces, blocks, held, sems, columns):
    rows = pieces[0].shape[2]
    copies = []
    for piece in range(PIECES):
        own, first, second = piece >> 2, (piece >> 1) & 1, piece & 1
        source = pieces[2 * own + second].at[first, :, :, columns]
        start = pl.multiple_of(blocks[piece] * rows, rows)
        copies.append(
            pltpu.make_async_copy(source, held.at[:, pl.ds(start, rows), :], sems.at[piece])
        )
    return copies


def part_copies(pieces, blocks, part, held, sems):
    rows = pieces[0].shape[2]
    copies = []
    for piece in range(PIECES):
        own, first, second = piece >> 2, (piece >> 1) & 1, piece & 1
        source = pieces[2 * own + second].at[first, part]
        start = pl.multiple_of(blocks[piece] * rows, rows)
        copies.append(
            pltpu.make_async_copy(source, held.at[pl.ds(start, rows), :], sems.at[piece])
        )
    return copies


def grad_copies(held, outs, blocks, columns, sems):
    rows = outs[0].shape[3]
    copies = []
    for piece in range(PIECES):
        own, first, second = piece >> 2, (piece >> 1) & 1, piece & 1
        target = outs[own].at[first, second, :, :, columns]
        start = pl.multiple_of(blocks[piece] * rows, rows)
        copies.append(
            pltpu.make_async_copy(held.at[:, pl.ds(start, rows), :], target, sems.at[piece])
        )
    return copies


def grad_part_copies(held, outs, blocks, part, sems):
    rows = outs[0].shape[3]
    copies = []
    for piece in range(PIECES):
        own, first, second = piece >> 2, (piece >> 1) & 1, piece & 1
        target = outs[own].at[first, second, part]
        start = pl.multiple_of(blocks[piece] * rows, rows)
        copies.append(
            pltpu.make_async_copy(held.at[pl.ds(start, rows), :], target, sems.at[piece])
        )
    return copies


def start_all(copies):
    for copy in copies:
        copy.start()


def wait_all(copies):
    for copy in copies:
        copy.wait()


def flat(block):
    return block.reshape(block.shape[0] * block.shape[1], block.shape[2])


def inverse_rms(rows):
    return lax.rsqrt(jnp.mean(rows * rows, axis=-1, keepdims=True) + EPSILON)


def qkv_kernel(blocks, frames, p0, p1, p2, p3, hidden, qkv, gains, held, gain_held, sems):
    step = pl.program_id(0)
    pieces = (p0, p1, p2, p3)
    width = frames.shape[1]

    def copies(part):
        return piece_copies(
            pieces, blocks, held.at[part], sems.at[part], pl.ds(part * width, width)
        )

    @pl.when(step == 0)
    def _():
        gain_copies = piece_copies(
            pieces, blocks, gain_held, sems.at[3], pl.ds(4 * width, LANES)
        )
        start_all(gain_copies)
        for part in range(3):
            start_all(copies(part))
        wait_all(gain_copies)
        across = flat(gain_held[...]).astype(F32).T
        gains[...] = across[:8]
        rows = frames[...].astype(F32)
        hidden[...] = (rows * inverse_rms(rows) * across[0:1]).astype(BF16)
        wait_all(copies(0))

    for part in (1, 2):

        @pl.when(step == part)
        def _():
            wait_all(copies(part))

    result = mxu(hidden[...], flat(held[step]))
    scale = jnp.where(step == 0, FACTOR, 1.0)
    qkv[...] = (result.astype(BF16).astype(F32) * scale).astype(BF16)


def qkv_call(blocks, frames, pieces):
    rows, width = frames.shape
    return pl.pallas_call(
        qkv_kernel,
        grid=(3,),
        in_specs=[SMEM_SPEC, whole((rows, width))] + [HBM_SPEC] * 4,
        out_specs=[
            whole((rows, width)),
            pl.BlockSpec((rows, width), lambda j: (0, j)),
            whole((8, width)),
        ],
        out_shape=[
            jax.ShapeDtypeStruct((rows, width), BF16),
            jax.ShapeDtypeStruct((rows, 3 * width), BF16),
            jax.ShapeDtypeStruct((8, width), F32),
        ],
        scratch_shapes=[
            pltpu.VMEM((3, Z_PARTS, width // Z_PARTS, width), BF16),
            pltpu.VMEM((Z_PARTS, width // Z_PARTS, LANES), BF16),
            pltpu.SemaphoreType.DMA((4, PIECES)),
        ],
        compiler_params=params(),
        cost_estimate=pl.CostEstimate(
            flops=6 * rows * width * width, bytes_accessed=10 * width * width, transcendentals=0
        ),
        name="qkv",
    )(blocks, frames, *pieces)


def attend_kernel(length, queries, keys, values, mixed, log_totals):
    pair = pl.program_id(0)
    rows = queries.shape[0]
    chunk = min(rows, 256)
    bias = jnp.where(
        lax.broadcasted_iota(jnp.int32, (1, rows), 1) < length[0], 0.0, -1e30
    ).astype(F32)
    lane = lax.broadcasted_iota(jnp.int32, (chunk, LANES), 1)

    @pl.when(pair == 0)
    def _():
        log_totals[...] = jnp.zeros_like(log_totals)

    for at in range(0, rows, chunk):
        here = pl.ds(at, chunk)
        part = queries[here, :]
        logs = log_totals[here, :]
        outs = []
        for half in range(2):
            query = jnp.where((lane < HEAD_DIM) == (half == 0), part, jnp.zeros_like(part))
            scores = mxu(query, keys[...], NT) + bias
            peak = jnp.max(scores, axis=-1, keepdims=True)
            expon = jnp.exp(scores - peak)
            sums = jnp.sum(expon, axis=-1, keepdims=True)
            shares = (expon * (1.0 / sums)).astype(BF16)
            outs.append(mxu(shares, values[...]))
            logs = jnp.where(lane == 2 * pair + half, peak + jnp.log(sums), logs)
        mixed[here, :] = jnp.where(lane < HEAD_DIM, outs[0], outs[1]).astype(BF16)
        log_totals[here, :] = logs


def attend_call(length, qkv):
    rows, width = qkv.shape[0], qkv.shape[1] // 3
    pairs = width // LANES
    return pl.pallas_call(
        attend_kernel,
        grid=(pairs,),
        in_specs=[
            SMEM_SPEC,
            pl.BlockSpec((rows, LANES), lambda h: (0, h)),
            pl.BlockSpec((rows, LANES), lambda h: (0, pairs + h)),
            pl.BlockSpec((rows, LANES), lambda h: (0, 2 * pairs + h)),
        ],
        out_specs=[pl.BlockSpec((rows, LANES), lambda h: (0, h)), whole((rows, LANES))],
        out_shape=[
            jax.ShapeDtypeStruct((rows, width), BF16),
            jax.ShapeDtypeStruct((rows, LANES), F32),
        ],
        compiler_params=params(),
        cost_estimate=pl.CostEstimate(
            flops=16 * rows * rows * width,
            bytes_accessed=8 * rows * width,
            transcendentals=HEADS * rows * rows,
        ),
        name="attend",
    )(length, qkv, qkv, qkv)


def out_kernel(blocks, frames, mixed, gains, p0, p1, p2, p3, middle, second, held, sems):
    width = frames.shape[1]
    copies = piece_copies((p0, p1, p2, p3), blocks, held, sems, pl.ds(3 * width, width))
    start_all(copies)
    wait_all(copies)
    result = frames[...].astype(F32) + mxu(mixed[...], flat(held[...]))
    middle[...] = result
    second[...] = (result * inverse_rms(result) * gains[1:2, :]).astype(BF16)


def out_call(blocks, frames, mixed, gains, pieces):
    rows, width = frames.shape
    return pl.pallas_call(
        out_kernel,
        grid=(1,),
        in_specs=[SMEM_SPEC, whole((rows, width)), whole((rows, width)), whole((8, width))]
        + [HBM_SPEC] * 4,
        out_specs=[whole((rows, width)), whole((rows, width))],
        out_shape=[
            jax.ShapeDtypeStruct((rows, width), F32),
            jax.ShapeDtypeStruct((rows, width), BF16),
        ],
        scratch_shapes=[
            pltpu.VMEM((Z_PARTS, width // Z_PARTS, width), BF16),
            pltpu.SemaphoreType.DMA((PIECES,)),
        ],
        compiler_params=params(),
        cost_estimate=pl.CostEstimate(
            flops=2 * rows * width * width, bytes_accessed=6 * width * width, transcendentals=0
        ),
        name="outward",
    )(blocks, frames, mixed, gains, *pieces)


def up_kernel(
    blocks, second, branch, p0, p1, p2, p3, upward, active, own, other,
    held, grads, sems, grad_sems,
):
    step = pl.program_id(0)
    steps = Z_PARTS
    slot = lax.rem(step, 2)
    pieces = (p0, p1, p2, p3)
    columns = held.shape[3]

    def copies(part):
        return piece_copies(
            pieces, blocks, held.at[part], sems.at[part], pl.ds(part * columns, columns)
        )

    def leave(part, at):
        return grad_part_copies(grads.at[at], (own, other), blocks, part, grad_sems.at[at])

    @pl.when(step == 0)
    def _():
        for part in range(steps):
            start_all(copies(part))

    for part in range(steps):

        @pl.when(step == part)
        def _():
            wait_all(copies(part))

    value = mxu(second[...], flat(held[step]))
    upward[...] = value
    bent = 0.5 * value * (1.0 + jnp.tanh(GELU_A * (value + GELU_B * value * value * value)))
    active[...] = bent.astype(BF16)

    @pl.when(step >= 2)
    def _():
        wait_all(leave(step - 2, slot))

    grads[slot] = mxu(active[...], branch[...], TN).astype(BF16)
    start_all(leave(step, slot))

    @pl.when(step == steps - 1)
    def _():
        wait_all(leave(step - 1, 1 - slot))
        wait_all(leave(step, slot))


def up_call(blocks, second, branch, pieces):
    rows, width = second.shape
    inner = pieces[0].shape[3]
    columns = inner // Z_PARTS
    part_rows = inner // (Z_PARTS * PIECES)
    grad = jax.ShapeDtypeStruct((2, 2, Z_PARTS, part_rows, width), BF16)
    return pl.pallas_call(
        up_kernel,
        grid=(Z_PARTS,),
        in_specs=[SMEM_SPEC, whole((rows, width)), whole((rows, width))] + [HBM_SPEC] * 4,
        out_specs=[
            pl.BlockSpec((rows, columns), lambda j: (0, j)),
            pl.BlockSpec((rows, columns), lambda j: (0, j)),
            HBM_SPEC,
            HBM_SPEC,
        ],
        out_shape=[
            jax.ShapeDtypeStruct((rows, inner), F32),
            jax.ShapeDtypeStruct((rows, inner), BF16),
            grad,
            grad,
        ],
        scratch_shapes=[
            pltpu.VMEM((Z_PARTS, Z_PARTS, width // Z_PARTS, columns), BF16),
            pltpu.VMEM((2, columns, width), BF16),
            pltpu.SemaphoreType.DMA((Z_PARTS, PIECES)),
            pltpu.SemaphoreType.DMA((2, PIECES)),
        ],
        compiler_params=params(),
        cost_estimate=pl.CostEstimate(
            flops=4 * rows * width * inner,
            bytes_accessed=4 * width * inner + 6 * rows * inner,
            transcendentals=rows * inner,
        ),
        name="upward",
    )(blocks, second, branch, *pieces)


def down_kernel(
    blocks, branch, second, upward, p0, p1, p2, p3, grad_upward, own, other,
    held, grads, sems, grad_sems,
):
    step = pl.program_id(0)
    steps = Z_PARTS
    slot = lax.rem(step, 2)
    pieces = (p0, p1, p2, p3)
    columns = upward.shape[1]

    def copies(part):
        return part_copies(pieces, blocks, part, held.at[part], sems.at[part])

    def leave(part, at):
        start = pl.multiple_of(part * columns, columns)
        return grad_copies(
            grads.at[at], (own, other), blocks, pl.ds(start, columns), grad_sems.at[at]
        )

    @pl.when(step == 0)
    def _():
        for part in range(steps):
            start_all(copies(part))

    for part in range(steps):

        @pl.when(step == part)
        def _():
            wait_all(copies(part))

    grad_active = mxu(branch[...], held[step], NT)
    value = upward[...]
    square = value * value
    bend = jnp.tanh(GELU_A * value * (1.0 + GELU_B * square))
    slope = 0.5 * (1.0 + bend) + 0.5 * value * (1.0 - bend * bend) * (
        GELU_A * (1.0 + 3.0 * GELU_B * square)
    )
    grad_upward[...] = (grad_active * slope).astype(BF16)

    @pl.when(step >= 2)
    def _():
        wait_all(leave(step - 2, slot))

    grad = mxu(second[...], grad_upward[...], TN).astype(BF16)
    grads[slot] = grad.reshape(grads.shape[1:])
    start_all(leave(step, slot))

    @pl.when(step == steps - 1)
    def _():
        wait_all(leave(step - 1, 1 - slot))
        wait_all(leave(step, slot))


def down_call(blocks, branch, second, upward, pieces):
    rows, width = second.shape
    inner = upward.shape[1]
    columns = inner // Z_PARTS
    grad = jax.ShapeDtypeStruct((2, 2, Z_PARTS, width // (Z_PARTS * PIECES), inner), BF16)
    return pl.pallas_call(
        down_kernel,
        grid=(Z_PARTS,),
        in_specs=[
            SMEM_SPEC,
            whole((rows, width)),
            whole((rows, width)),
            pl.BlockSpec((rows, columns), lambda j: (0, j)),
        ]
        + [HBM_SPEC] * 4,
        out_specs=[pl.BlockSpec((rows, columns), lambda j: (0, j)), HBM_SPEC, HBM_SPEC],
        out_shape=[jax.ShapeDtypeStruct((rows, inner), BF16), grad, grad],
        scratch_shapes=[
            pltpu.VMEM((Z_PARTS, columns, width), BF16),
            pltpu.VMEM((2, Z_PARTS, width // Z_PARTS, columns), BF16),
            pltpu.SemaphoreType.DMA((Z_PARTS, PIECES)),
            pltpu.SemaphoreType.DMA((2, PIECES)),
        ],
        compiler_params=params(),
        cost_estimate=pl.CostEstimate(
            flops=4 * rows * width * inner,
            bytes_accessed=4 * width * inner + 6 * rows * inner,
            transcendentals=rows * inner,
        ),
        name="downward",
    )(blocks, branch, second, upward, *pieces)


def result_kernel(blocks, length, middle, active, p0, p1, p2, p3, output, held, sums, sems):
    step = pl.program_id(0)
    steps = Z_PARTS
    pieces = (p0, p1, p2, p3)

    def copies(part):
        return part_copies(pieces, blocks, part, held.at[part], sems.at[part])

    @pl.when(step == 0)
    def _():
        for part in range(steps):
            start_all(copies(part))
        sums[...] = middle[...]

    for part in range(steps):

        @pl.when(step == part)
        def _():
            wait_all(copies(part))

    sums[...] += mxu(active[...], held[step])

    @pl.when(step == steps - 1)
    def _():
        valid = lax.broadcasted_iota(jnp.int32, (sums.shape[0], 1), 0) < length[0]
        output[...] = (sums[...] * valid.astype(F32)).astype(BF16)


def result_call(blocks, length, middle, active, pieces):
    rows, width = middle.shape
    inner = active.shape[1]
    columns = inner // Z_PARTS
    return pl.pallas_call(
        result_kernel,
        grid=(Z_PARTS,),
        in_specs=[
            SMEM_SPEC,
            SMEM_SPEC,
            whole((rows, width)),
            pl.BlockSpec((rows, columns), lambda j: (0, j)),
        ]
        + [HBM_SPEC] * 4,
        out_specs=whole((rows, width)),
        out_shape=jax.ShapeDtypeStruct((rows, width), BF16),
        scratch_shapes=[
            pltpu.VMEM((Z_PARTS, columns, width), BF16),
            pltpu.VMEM((rows, width), F32),
            pltpu.SemaphoreType.DMA((Z_PARTS, PIECES)),
        ],
        compiler_params=params(),
        cost_estimate=pl.CostEstimate(
            flops=2 * rows * width * inner, bytes_accessed=3 * width * inner, transcendentals=0
        ),
        name="result",
    )(blocks, length, middle, active, *pieces)


def middle_kernel(
    blocks, branch, middle, gains, grad_upward, u0, u1, u2, u3, p0, p1, p2, p3,
    grad_middle, grad_attn, grad_mixed, held, out_held, sums, sems, out_sems,
):
    step = pl.program_id(0)
    steps = Z_PARTS
    width = middle.shape[1]
    columns = grad_upward.shape[1]

    def copies(part):
        return piece_copies(
            (u0, u1, u2, u3), blocks, held.at[part], sems.at[part], pl.ds(part * columns, columns)
        )

    out_copies = piece_copies(
        (p0, p1, p2, p3), blocks, out_held, out_sems, pl.ds(3 * width, width)
    )

    @pl.when(step == 0)
    def _():
        for part in range(steps):
            start_all(copies(part))
        start_all(out_copies)
        sums[...] = jnp.zeros_like(sums)

    for part in range(steps):

        @pl.when(step == part)
        def _():
            wait_all(copies(part))

    sums[...] += mxu(grad_upward[...], flat(held[step]), NT)

    @pl.when(step == steps - 1)
    def _():
        rows = middle[...]
        inverse = inverse_rms(rows)
        normal = rows * inverse
        scaled = sums[...] * gains[1:2, :]
        mean = jnp.mean(scaled * normal, axis=-1, keepdims=True)
        result = branch[...].astype(F32) + inverse * (scaled - normal * mean)
        grad_middle[...] = result
        low = result.astype(BF16)
        grad_attn[...] = low
        wait_all(out_copies)
        grad_mixed[...] = mxu(low, flat(out_held[...]), NT).astype(BF16)


def middle_call(blocks, branch, middle, gains, grad_upward, up_pieces, pieces):
    rows, width = middle.shape
    inner = grad_upward.shape[1]
    columns = inner // Z_PARTS
    return pl.pallas_call(
        middle_kernel,
        grid=(Z_PARTS,),
        in_specs=[
            SMEM_SPEC,
            whole((rows, width)),
            whole((rows, width)),
            whole((8, width)),
            pl.BlockSpec((rows, columns), lambda j: (0, j)),
        ]
        + [HBM_SPEC] * 8,
        out_specs=[whole((rows, width))] * 3,
        out_shape=[
            jax.ShapeDtypeStruct((rows, width), F32),
            jax.ShapeDtypeStruct((rows, width), BF16),
            jax.ShapeDtypeStruct((rows, width), BF16),
        ],
        scratch_shapes=[
            pltpu.VMEM((Z_PARTS, Z_PARTS, width // Z_PARTS, columns), BF16),
            pltpu.VMEM((Z_PARTS, width // Z_PARTS, width), BF16),
            pltpu.VMEM((rows, width), F32),
            pltpu.SemaphoreType.DMA((Z_PARTS, PIECES)),
            pltpu.SemaphoreType.DMA((PIECES,)),
        ],
        compiler_params=params(),
        cost_estimate=pl.CostEstimate(
            flops=2 * rows * width * (inner + width),
            bytes_accessed=3 * width * inner,
            transcendentals=0,
        ),
        name="middle",
    )(blocks, branch, middle, gains, grad_upward, *up_pieces, *pieces)


def attend_back_kernel(length, queries, keys, values, log_totals, grads, grad_qkv, across):
    pair = pl.program_id(0)
    rows = queries.shape[0]
    bias = jnp.where(
        lax.broadcasted_iota(jnp.int32, (rows, 1), 0) < length[0], 0.0, -1e30
    ).astype(F32)
    lane = lax.broadcasted_iota(jnp.int32, (rows, LANES), 1)

    @pl.when(pair == 0)
    def _():
        across[...] = log_totals[...].T

    query, key, value, grad = queries[...], keys[...], values[...], grads[...]
    parts = []
    for half in range(2):
        mine = (lane < HEAD_DIM) == (half == 0)
        query_half = jnp.where(mine, query, jnp.zeros_like(query))
        grad_half = jnp.where(mine, grad, jnp.zeros_like(grad))
        scores = mxu(key, query_half, NT) + bias
        chance = jnp.exp(scores - across[pl.ds(2 * pair + half, 1), :])
        grad_value = mxu(chance.astype(BF16), grad)
        grad_chance = mxu(value, grad_half, NT)
        mean = jnp.sum(chance * grad_chance, axis=0, keepdims=True)
        grad_scores = (chance * (grad_chance - mean)).astype(BF16)
        grad_key = mxu(grad_scores, query)
        grad_query = mxu(grad_scores, key, TN) * FACTOR
        parts.append((grad_query, grad_key, grad_value))
    for place in range(3):
        grad_qkv[place] = jnp.where(lane < HEAD_DIM, parts[0][place], parts[1][place]).astype(BF16)


def attend_back_call(length, qkv, log_totals, grad_mixed):
    rows, width = grad_mixed.shape
    pairs = width // LANES
    return pl.pallas_call(
        attend_back_kernel,
        grid=(pairs,),
        in_specs=[
            SMEM_SPEC,
            pl.BlockSpec((rows, LANES), lambda h: (0, h)),
            pl.BlockSpec((rows, LANES), lambda h: (0, pairs + h)),
            pl.BlockSpec((rows, LANES), lambda h: (0, 2 * pairs + h)),
            whole((rows, LANES)),
            pl.BlockSpec((rows, LANES), lambda h: (0, h)),
        ],
        out_specs=pl.BlockSpec((3, rows, LANES), lambda h: (0, 0, h)),
        out_shape=jax.ShapeDtypeStruct((3, rows, width), BF16),
        scratch_shapes=[pltpu.VMEM((LANES, rows), F32)],
        compiler_params=params(),
        cost_estimate=pl.CostEstimate(
            flops=40 * rows * rows * width,
            bytes_accessed=14 * rows * width,
            transcendentals=HEADS * rows * rows,
        ),
        name="attend_back",
    )(length, qkv, qkv, qkv, log_totals, grad_mixed)


def attn_grad_kernel(
    blocks, hidden, mixed, grad_qkv, grad_attn, own, other, grads, grad_sems
):
    step = pl.program_id(0)
    steps = 4
    slot = lax.rem(step, 2)
    width = hidden.shape[1]

    def leave(part, at):
        start = pl.multiple_of(part * width, width)
        return grad_copies(
            grads.at[at], (own, other), blocks, pl.ds(start, width), grad_sems.at[at]
        )

    @pl.when(step >= 2)
    def _():
        wait_all(leave(step - 2, slot))

    @pl.when(step < 3)
    def _():
        grad = mxu(hidden[...], grad_qkv[0], TN).astype(BF16)
        grads[slot] = grad.reshape(grads.shape[1:])

    @pl.when(step == 3)
    def _():
        grad = mxu(mixed[...], grad_attn[...], TN).astype(BF16)
        grads[slot] = grad.reshape(grads.shape[1:])

    start_all(leave(step, slot))

    @pl.when(step == steps - 1)
    def _():
        wait_all(leave(step - 1, 1 - slot))
        wait_all(leave(step, slot))


def attn_grad_call(blocks, hidden, mixed, grad_qkv, grad_attn):
    rows, width = hidden.shape
    grad = jax.ShapeDtypeStruct((2, 2, Z_PARTS, width // (Z_PARTS * PIECES), 4 * width), BF16)
    return pl.pallas_call(
        attn_grad_kernel,
        grid=(4,),
        in_specs=[
            SMEM_SPEC,
            whole((rows, width)),
            whole((rows, width)),
            pl.BlockSpec((1, rows, width), lambda j: (jnp.minimum(j, 2), 0, 0)),
            whole((rows, width)),
        ],
        out_specs=[HBM_SPEC, HBM_SPEC],
        out_shape=[grad, grad],
        scratch_shapes=[
            pltpu.VMEM((2, Z_PARTS, width // Z_PARTS, width), BF16),
            pltpu.SemaphoreType.DMA((2, PIECES)),
        ],
        compiler_params=params(),
        cost_estimate=pl.CostEstimate(
            flops=8 * rows * width * width,
            bytes_accessed=8 * width * width + 12 * rows * width,
            transcendentals=0,
        ),
        name="attn_grads",
    )(blocks, hidden, mixed, grad_qkv, grad_attn)


def frames_kernel(
    blocks, frames, gains, grad_middle, grad_qkv, p0, p1, p2, p3, grad_frames, held, sums, sems
):
    step = pl.program_id(0)
    width = frames.shape[1]

    def copies(part):
        return piece_copies(
            (p0, p1, p2, p3), blocks, held.at[part], sems.at[part], pl.ds(part * width, width)
        )

    @pl.when(step == 0)
    def _():
        for part in range(3):
            start_all(copies(part))
        sums[...] = jnp.zeros_like(sums)

    for part in range(3):

        @pl.when(step == part)
        def _():
            wait_all(copies(part))

    sums[...] += mxu(grad_qkv[0], flat(held[step]), NT)

    @pl.when(step == 2)
    def _():
        rows = frames[...].astype(F32)
        inverse = inverse_rms(rows)
        normal = rows * inverse
        scaled = sums[...] * gains[0:1, :]
        mean = jnp.mean(scaled * normal, axis=-1, keepdims=True)
        grad_frames[...] = grad_middle[...] + inverse * (scaled - normal * mean)


def frames_call(blocks, frames, gains, grad_middle, grad_qkv, pieces):
    rows, width = frames.shape
    return pl.pallas_call(
        frames_kernel,
        grid=(3,),
        in_specs=[
            SMEM_SPEC,
            whole((rows, width)),
            whole((8, width)),
            whole((rows, width)),
            pl.BlockSpec((1, rows, width), lambda j: (j, 0, 0)),
        ]
        + [HBM_SPEC] * 4,
        out_specs=whole((rows, width)),
        out_shape=jax.ShapeDtypeStruct((rows, width), F32),
        scratch_shapes=[
            pltpu.VMEM((3, Z_PARTS, width // Z_PARTS, width), BF16),
            pltpu.VMEM((rows, width), F32),
            pltpu.SemaphoreType.DMA((3, PIECES)),
        ],
        compiler_params=params(),
        cost_estimate=pl.CostEstimate(
            flops=6 * rows * width * width, bytes_accessed=10 * width * width, transcendentals=0
        ),
        name="frames_back",
    )(blocks, frames, gains, grad_middle, grad_qkv, *pieces)


def on_device(
    sizes, frames, lengths, w_query, w_key, w_value, w_out, w_up, w_down,
    gain_attn, gain_mlp, cotangent,
):
    width = frames.shape[-1]
    blocks = piece_blocks(sizes)
    rows_in = frames[0]
    valid = lax.broadcasted_iota(jnp.int32, (rows_in.shape[0], 1), 0) < lengths[0]
    branch = jnp.where(valid, cotangent[0], jnp.zeros_like(cotangent[0]))
    gains = jnp.pad(jnp.stack((gain_attn, gain_mlp), axis=1), ((0, 0), (0, LANES - 2)))
    attn = jnp.concatenate((w_query, w_key, w_value, w_out, gains), axis=1)
    attn_pieces = gather_pieces(attn, sizes)
    up_pieces = gather_pieces(w_up, sizes)
    down_pieces = gather_pieces(w_down, sizes)

    hidden, qkv, gain_rows = qkv_call(blocks, rows_in, attn_pieces)
    mixed, log_totals = attend_call(lengths, qkv)
    middle, second = out_call(blocks, rows_in, mixed, gain_rows, attn_pieces)
    upward, active, down_own, down_other = up_call(blocks, second, branch, up_pieces)
    down_rows = scatter_pieces(down_own, down_other, sizes)
    grad_upward, up_own, up_other = down_call(blocks, branch, second, upward, down_pieces)
    up_rows = scatter_pieces(up_own, up_other, sizes)
    grad_middle, grad_attn, grad_mixed = middle_call(
        blocks, branch, middle, gain_rows, grad_upward, up_pieces, attn_pieces
    )
    grad_qkv = attend_back_call(lengths, qkv, log_totals, grad_mixed)
    attn_own, attn_other = attn_grad_call(blocks, hidden, mixed, grad_qkv, grad_attn)
    attn_rows = scatter_pieces(attn_own, attn_other, sizes)
    output = result_call(blocks, lengths, middle, active, down_pieces)
    grad_frames = frames_call(blocks, rows_in, gain_rows, grad_middle, grad_qkv, attn_pieces)

    grad_query = attn_rows[:, :width]
    grad_key = attn_rows[:, width : 2 * width]
    grad_value = attn_rows[:, 2 * width : 3 * width]
    grad_out = attn_rows[:, 3 * width :]
    gain_one = (
        jnp.sum(w_query.astype(F32) * grad_query, axis=1)
        + jnp.sum(w_key.astype(F32) * grad_key, axis=1)
        + jnp.sum(w_value.astype(F32) * grad_value, axis=1)
    ) / gain_attn.astype(F32)
    gain_two = jnp.sum(w_up.astype(F32) * up_rows, axis=1) / gain_mlp.astype(F32)
    return (
        output[None], grad_frames[None], grad_query, grad_key, grad_value, grad_out,
        up_rows, down_rows, gain_one, gain_two,
    )


def solution(mesh):
    wide, narrow = mesh.shape["wide"], mesh.shape["narrow"]
    y = 1
    while 4 * y * y <= wide:
        y *= 2
    sizes = {"z": wide // y, "y": y, "x": narrow // 2, "c": 2}
    fine = Mesh(mesh.devices.reshape(tuple(sizes[name] for name in ALL)), ALL)
    split = P(ALL)
    return jax.shard_map(
        functools.partial(on_device, sizes),
        mesh=fine,
        in_specs=(split,) * 11,
        out_specs=(split,) * 10,
        check_vma=False,
    )
```

time: 1370 us -> 444 us (0.32)
  waiting for transfers between devices: 1070 us -> 228 us
  matrix products: 148 us -> 0 us
  Pallas kernels: 0 us -> 133 us
  blocking collectives: 81.9 us -> 0 us
  starting transfers between devices: 1.26 us -> 22.6 us
  other arithmetic: 23.9 us -> 37.7 us
    reduce_scatter x6 -> x3, waiting for transfers between devices: 777 us -> 13.5 us  [scatter_pieces(): lax.psum_scatter(mine, 'z', scatter_dimension=0, tiled=False).astype(F32)]
    all_gather x6 -> x3, waiting for transfers between devices: 292 us -> 82.6 us  [gather_pieces(): column = lax.all_gather(shard, 'z', axis=0, tiled=False)]
    dot_general x24 -> x0, matrix products: 148 us -> none  [the longest x1 15.1 us: on_device(): jnp.einsum('rf,rd->fd', active, grad_branch, preferred_element_type=jnp.f...]
    pallas_call x0 -> x10, Pallas kernels: none -> 133 us  [the longest x1 20.7 us: down_call(): pl.pallas_call(down_kernel, grid=(Z_PARTS,), in_specs=[SMEM_SPEC, whole((...]
    ppermute x0 -> x21, waiting for transfers between devices: none -> 132 us  [the longest x3 58.7 us: scatter_pieces(): near = lax.ppermute(away, PLANE, plane_pairs(1))]
    unnamed x2 -> x0, blocking collectives: 81.9 us -> none
    ppermute x0 -> x21, starting transfers between devices: none -> 22.1 us  [the longest x3 4.63 us: scatter_pieces(): near = lax.ppermute(away, PLANE, plane_pairs(1))]
    convert_element_type x4 -> x11, other arithmetic: 8.09 us -> 25.4 us  [the longest x3 9.88 us: scatter_pieces(): mine = total(own[0, 0], got[0, 0], near[0], far).astype(BF16)]
  transfers between devices with their start and end apart: 12 -> 27, of which waited for: 11 -> 13; matrix products, arithmetic and copies ran while one was open for 12% -> 8% of each run, Pallas kernels for 0% -> 25%
where the time goes in v2:
time: 444 us; the launch traced here: 443 us
  waiting for transfers between devices  228 us (51%)
  Pallas kernels  133 us (30%)
  other arithmetic  37.7 us (8%)
  starting transfers between devices  22.6 us (5%)
  between operations  15.1 us (3%)
  local copies, waits for them, and re-layouts  6.22 us (1%)
    all_gather x3, waiting for transfers between devices, gather_pieces(): column = lax.all_gather(shard, 'z', axis=0, tiled=False)  82.6 us
    ppermute x3, waiting for transfers between devices, scatter_pieces(): near = lax.ppermute(away, PLANE, plane_pairs(1))  58.7 us
    ppermute x3, waiting for transfers between devices, gather_pieces(): far = lax.ppermute(own, PLANE, plane_pairs(2))  32.3 us
    pallas_call x1, Pallas kernels, down_call(): pl.pallas_call(down_kernel, grid=(Z_PARTS,), in_specs=[SMEM_SPEC, whole((...  20.7 us
    ppermute x3, waiting for transfers between devices, gather_pieces(): near = lax.ppermute(column, PLANE, plane_pairs(1))  20.2 us
    pallas_call x1, Pallas kernels, up_call(): pl.pallas_call(up_kernel, grid=(Z_PARTS,), in_specs=[SMEM_SPEC, whole((ro...  18.7 us
    pallas_call x1, Pallas kernels, attend_back_call(): pl.pallas_call(attend_back_kernel, grid=(pairs,), in_specs=[SMEM_SPEC, pl...  17.5 us
    pallas_call x1, Pallas kernels, attend_call(): pl.pallas_call(attend_kernel, grid=(pairs,), in_specs=[SMEM_SPEC, pl.Bloc...  17.1 us
  transfers between devices with their start and end apart: 27, of which 13 were waited for; matrix products, arithmetic and copies ran while one was open for 8% of the time, Pallas kernels for 25%

profile of v2, /device:TPU:0, one launch (start us, length us, event | category | flops | bytes accessed | tf_op | source)
XLA Modules:
  0.0 443.1 jit_solution(10170143615397326499)
XLA Ops:
  12.9 30.5 %all-gather.7.cloned.1.call-done = bf16[128,4224]{1,0:T(8,128)(2,1)} async-done(((bf16[32,4224]{1,0:T(8,128)(2,1)}), bf16[128,4224]{1,0:T(8,128)(2,1)}) %all-gather.7.cloned.1.call-update) | async-done | bytes 1081360 | tf_op jit(solution)/shard_map/all_gather | solution.py:72
  43.5 1.5 collective-permute-start
  45.0 27.5 %all-gather.9.cloned.1.call-done = bf16[128,4096]{1,0:T(8,128)(2,1)} async-done(((bf16[32,4096]{1,0:T(8,128)(2,1)}), bf16[128,4096]{1,0:T(8,128)(2,1)}) %all-gather.9.cloned.1.call-update) | async-done | bytes 1048592 | tf_op jit(solution)/shard_map/all_gather | solution.py:72
  72.5 1.5 collective-permute-start.4
  74.0 1.5 pad_maximum_fusion.p0
  75.4 1.5 collective-permute-start.1
  77.0 24.6 %all-gather.11.cloned.1.call-done = bf16[512,1024]{1,0:T(8,128)(2,1)} async-done(((bf16[128,1024]{1,0:T(8,128)(2,1)}), bf16[512,1024]{1,0:T(8,128)(2,1)}) %all-gather.11.cloned.1.call-update) | async-done | bytes 1048592 | tf_op jit(solution)/shard_map/all_gather | solution.py:72
  101.5 1.5 collective-permute-start.8
  103.0 3.1 pad_maximum_fusion.1.p0.u0
  106.1 1.5 collective-permute-start.5
  107.6 20.2 %collective-permute-done.8 = bf16[4,128,1024]{2,1,0:T(8,128)(2,1)S(1)} collective-permute-done((bf16[4,128,1024]{2,1,0:T(8,128)(2,1)}, bf16[4,128,1024]{2,1,0:T(8,128)(2,1)S(1)}, u32[]{:S(2)}, u32[]{:S(2)}) %collective-permute-start.8) | collective-permute-done | bytes 1048608 | tf_op jit(solution)/shard_map/ppermute | solution.py:73
  127.8 1.5 pad_maximum_fusion.2.p0
  129.3 1.5 collective-permute-start.9
  131.3 11.9 %collective-permute-done.5.p1.u1 = bf16[2,4,32,4096]{3,2,1,0:T(8,128)(2,1)} collective-permute-done((bf16[2,4,32,4096]{3,2,1,0:T(8,128)(2,1)}, bf16[2,4,32,4096]{3,2,1,0:T(8,128)(2,1)}, u32[]{:S(2)}, u32[]{:S(2)}) %collective-permute-start.5) | collective-permute-done | bytes 2097184 | tf_op jit(solution)/shard_map/ppermute | solution.py:75
  145.2 20.4 %collective-permute-done.9.p1 = bf16[2,4,128,1024]{3,2,1,0:T(8,128)(2,1)} collective-permute-done((bf16[2,4,128,1024]{3,2,1,0:T(8,128)(2,1)}, bf16[2,4,128,1024]{3,2,1,0:T(8,128)(2,1)}, u32[]{:S(2)}, u32[]{:S(2)}) %collective-permute-start.9) | collective-permute-done | bytes 2097184 | tf_op jit(solution)/shard_map/ppermute | solution.py:75
  168.5 8.3 %qkv.1 = (bf16[512,1024]{1,0:T(8,128)(2,1)}, bf16[512,3072]{1,0:T(8,128)(2,1)}, f32[8,1024]{1,0:T(8,128)}) custom-call(s32[8]{0:T(128)} %multiply_add_fusion.blocks, bf16[512,1024]{1,0:T(8,128)(2,1)} %bitcast.76, bf16[2,4,32,4224]{3,2,1,0:T(8,128)(2,1)} %copy-done, bf16[2,4,32,4224]{3,2,1,0:T(8,128)(2,1)} %collective-permute-done.1.p1, ...), custom_call_target="tpu_custom_call" | custom-call | flops 3221225472 | bytes 10485760 | tf_op jit(solution)/shard_map/qkv/pallas_call | solution.py:221
  176.7 17.1 %attend.1 = (bf16[512,1024]{1,0:T(8,128)(2,1)}, f32[512,128]{1,0:T(8,128)}) custom-call(s32[1]{0:T(128)} %copy.27.length, bf16[512,3072]{1,0:T(8,128)(2,1)} %get-tuple-element.29.queries.keys.values, bf16[512,3072]{1,0:T(8,128)(2,1)} %get-tuple-element.29.queries.keys.values, bf16[512,3072]{1,0:T(8,128)(2,1)} %get-tuple-element.29.queries.keys.values), custom_call_target="tpu_custom_call" | custom-call | flops 4294967296 | bytes 4194304 | tf_op jit(solution)/shard_map/attend/pallas_call | solution.py:282
  193.9 6.1 %outward.1 = (f32[512,1024]{1,0:T(8,128)}, bf16[512,1024]{1,0:T(8,128)(2,1)}) custom-call(s32[8]{0:T(128)} %multiply_add_fusion.blocks, bf16[512,1024]{1,0:T(8,128)(2,1)} %bitcast.77, bf16[512,1024]{1,0:T(8,128)(2,1)} %get-tuple-element.30.mixed, f32[8,1024]{1,0:T(8,128)} %get-tuple-element.31.gains, bf16[2,4,32,4224]{3,2,1,0:T(8,128)(2,1)} %copy-done, ...), custom_call_target="tpu_custom_call" | custom-call | flops 1073741824 | bytes 6291456 | tf_op jit(solution)/shard_map/outward/pallas_call | solution.py:318
  200.0 18.7 %upward.1 = (f32[512,4096]{1,0:T(8,128)}, bf16[512,4096]{1,0:T(8,128)(2,1)}, bf16[2,2,4,128,1024]{4,3,2,1,0:T(8,128)(2,1)}, bf16[2,2,4,128,1024]{4,3,2,1,0:T(8,128)(2,1)}) custom-call(s32[8]{0:T(128)} %multiply_add_fusion.blocks, bf16[512,1024]{1,0:T(8,128)(2,1)} %get-tuple-element.33.second, bf16[512,1024]{1,0:T(8,128)(2,1)} %bitcast_select_fusion.branch, ...), custom_call_target="tpu_custom_call" | custom-call | flops 8589934592 | bytes 29360128 | tf_op jit(solution)/shard_map/upward/pallas_call | solution.py:393
  220.8 20.7 %downward.1 = (bf16[512,4096]{1,0:T(8,128)(2,1)}, bf16[2,2,4,32,4096]{4,3,2,1,0:T(8,128)(2,1)}, bf16[2,2,4,32,4096]{4,3,2,1,0:T(8,128)(2,1)}) custom-call(s32[8]{0:T(128)} %multiply_add_fusion.blocks, bf16[512,1024]{1,0:T(8,128)(2,1)} %bitcast_select_fusion.branch, bf16[512,1024]{1,0:T(8,128)(2,1)} %get-tuple-element.33.second, ...), custom_call_target="tpu_custom_call" | custom-call | flops 8589934592 | bytes 29360128 | tf_op jit(solution)/shard_map/downward/pallas_call | solution.py:483
  242.1 14.0 %middle.1 = (f32[512,1024]{1,0:T(8,128)}, bf16[512,1024]{1,0:T(8,128)(2,1)}, bf16[512,1024]{1,0:T(8,128)(2,1)}) custom-call(s32[8]{0:T(128)} %multiply_add_fusion.blocks, bf16[512,1024]{1,0:T(8,128)(2,1)} %bitcast_select_fusion.branch, f32[512,1024]{1,0:T(8,128)} %get-tuple-element.32.middle, f32[8,1024]{1,0:T(8,128)} %get-tuple-element.31.gains, ...), custom_call_target="tpu_custom_call" | custom-call | flops 5368709120 | bytes 12582912 | tf_op jit(solution)/shard_map/middle/pallas_call | solution.py:620
  256.1 17.5 %attend_back.1.grad_qkv = bf16[3,512,1024]{2,1,0:T(8,128)(2,1)} custom-call(s32[1]{0:T(128)} %copy.27.length, bf16[512,3072]{1,0:T(8,128)(2,1)} %get-tuple-element.29.queries.keys.values, bf16[512,3072]{1,0:T(8,128)(2,1)} %get-tuple-element.29.queries.keys.values, bf16[512,3072]{1,0:T(8,128)(2,1)} %get-tuple-element.29.queries.keys.values, ...), custom_call_target="tpu_custom_call" | custom-call | flops 10737418240 | bytes 7340032 | tf_op jit(solution)/shard_map/attend_back/pallas_call | solution.py:688
  273.6 10.0 %attn_grads.1 = (bf16[2,2,4,32,4096]{4,3,2,1,0:T(8,128)(2,1)}, bf16[2,2,4,32,4096]{4,3,2,1,0:T(8,128)(2,1)}) custom-call(s32[8]{0:T(128)} %multiply_add_fusion.blocks, bf16[512,1024]{1,0:T(8,128)(2,1)} %get-tuple-element.40.hidden, bf16[512,1024]{1,0:T(8,128)(2,1)} %get-tuple-element.30.mixed, bf16[3,512,1024]{2,1,0:T(8,128)(2,1)} %attend_back.1.grad_qkv, ...), custom_call_target="tpu_custom_call" | custom-call | flops 4294967296 | bytes 14680064 | tf_op jit(solution)/shard_map/attn_grads/pallas_call | solution.py:751
  284.2 2.5 fusion.1
  286.7 1.5 collective-permute-start.16
  288.3 6.5 %collective-permute-done.12 = bf16[2,2,4,32,4096]{4,3,2,1,0:T(8,128)(2,1)S(1)} collective-permute-done((bf16[2,2,4,32,4096]{4,3,2,1,0:T(8,128)(2,1)}, bf16[2,2,4,32,4096]{4,3,2,1,0:T(8,128)(2,1)S(1)}, u32[]{:S(2)}, u32[]{:S(2)}) %collective-permute-start.12) | collective-permute-done | bytes 4194336 | tf_op jit(solution)/shard_map/ppermute | solution.py:92
  295.6 1.5 collective-permute-start.13
  297.2 15.7 %collective-permute-done.16 = bf16[2,4,32,4096]{3,2,1,0:T(8,128)(2,1)S(1)} collective-permute-done((bf16[2,4,32,4096]{3,2,1,0:T(8,128)(2,1)S(1)}, bf16[2,4,32,4096]{3,2,1,0:T(8,128)(2,1)S(1)}, u32[]{:S(2)}, u32[]{:S(2)}) %collective-permute-start.16) | collective-permute-done | bytes 2097184 | tf_op jit(solution)/shard_map/ppermute | solution.py:94
  312.8 1.7 fusion.6
  314.5 1.5 collective-permute-start.17
  316.1 30.5 %collective-permute-done.13 = bf16[2,4,32,4096]{3,2,1,0:T(8,128)(2,1)S(1)} collective-permute-done((bf16[2,4,32,4096]{3,2,1,0:T(8,128)(2,1)S(1)}, bf16[2,4,32,4096]{3,2,1,0:T(8,128)(2,1)S(1)}, u32[]{:S(2)}, u32[]{:S(2)}) %collective-permute-start.13) | collective-permute-done | bytes 2097184 | tf_op jit(solution)/shard_map/ppermute | solution.py:94
  346.6 1.7 fusion.9
  348.2 1.5 collective-permute-start.14
  349.7 2.9 fusion.8
  352.9 3.4 fusion.2
  356.3 1.6 collective-permute-start.19
  357.8 10.6 %collective-permute-done.14 = bf16[4,32,4096]{2,1,0:T(8,128)(2,1)S(1)} collective-permute-done((bf16[4,32,4096]{2,1,0:T(8,128)(2,1)}, bf16[4,32,4096]{2,1,0:T(8,128)(2,1)S(1)}, u32[]{:S(2)}, u32[]{:S(2)}) %collective-permute-start.14) | collective-permute-done | bytes 1048608 | tf_op jit(solution)/shard_map/ppermute | solution.py:96
  368.4 3.2 fusion.11
  371.7 12.5 %collective-permute-done.19 = bf16[2,4,128,1024]{3,2,1,0:T(8,128)(2,1)} collective-permute-done((bf16[2,4,128,1024]{3,2,1,0:T(8,128)(2,1)S(1)}, bf16[2,4,128,1024]{3,2,1,0:T(8,128)(2,1)}, u32[]{:S(2)}, u32[]{:S(2)}) %collective-permute-start.19) | collective-permute-done | bytes 2097184 | tf_op jit(solution)/shard_map/ppermute | solution.py:94
  384.2 2.7 fusion.3
  386.9 1.5 collective-permute-start.20
  388.4 10.1 %result.1 = bf16[512,1024]{1,0:T(8,128)(2,1)} custom-call(s32[8]{0:T(128)} %multiply_add_fusion.blocks, s32[1]{0:T(128)} %copy.27.length, f32[512,1024]{1,0:T(8,128)} %get-tuple-element.32.middle, bf16[512,4096]{1,0:T(8,128)(2,1)} %get-tuple-element.34.active, bf16[2,4,128,1024]{3,2,1,0:T(8,128)(2,1)} %pad_maximum_fusion.2.p0, ...), custom_call_target="tpu_custom_call" | custom-call | flops 4294967296 | bytes 12582912 | tf_op jit(solution)/shard_map/result/pallas_call | solution.py:543
  398.5 3.2 collective-permute-done.20
  401.8 3.8 fusion.5
  405.6 10.4 %frames_back.1 = f32[512,1024]{1,0:T(8,128)} custom-call(s32[8]{0:T(128)} %multiply_add_fusion.blocks, bf16[512,1024]{1,0:T(8,128)(2,1)} %bitcast.78, f32[8,1024]{1,0:T(8,128)} %get-tuple-element.31.gains, f32[512,1024]{1,0:T(8,128)} %get-tuple-element.37.grad_middle, bf16[3,512,1024]{2,1,0:T(8,128)(2,1)} %attend_back.1.grad_qkv, ...), custom_call_target="tpu_custom_call" | custom-call | flops 3221225472 | bytes 10485760 | tf_op jit(solution)/shard_map/frames_back/pallas_call | solution.py:814
  416.1 1.9 multiply_reduce_fusion
  421.0 13.5 %reduce-scatter.8.cloned.1.call-done = bf16[1,128,1024]{2,1,0:T(8,128)(2,1)} async-done(((bf16[4,128,1024]{2,1,0:T(8,128)(2,1)}), bf16[1,128,1024]{2,1,0:T(8,128)(2,1)}) %reduce-scatter.8.cloned.1.call-update) | async-done | bytes 262160 | tf_op jit(solution)/shard_map/reduce_scatter | solution.py:98
  434.5 1.8 bitcast_convert_fusion
  (84 shorter events, 17.8 us)
Async XLA Ops:
  7.2 36.3 %all-gather.7.cloned.1.call-start = ((), (), s32[]{:S(2)}) async-start(), calls=%async_computation.6 | async-start | bytes 1351680 | tf_op jit(solution)/shard_map/all_gather | solution.py:72
  11.4 0.7 copy-start.9
  12.1 60.3 %all-gather.9.cloned.1.call-start = ((), (), s32[]{:S(2)}) async-start(), calls=%async_computation.7 | async-start | bytes 1310720 | tf_op jit(solution)/shard_map/all_gather | solution.py:72
  12.9 88.6 %all-gather.11.cloned.1.call-start = ((), (), s32[]{:S(2)}) async-start(), calls=%async_computation.8 | async-start | bytes 1310720 | tf_op jit(solution)/shard_map/all_gather | solution.py:72
  43.5 30.5 %collective-permute-start = (bf16[4,32,4224]{2,1,0:T(8,128)(2,1)}, bf16[4,32,4224]{2,1,0:T(8,128)(2,1)S(1)}, u32[]{:S(2)}, u32[]{:S(2)}) collective-permute-start(bf16[4,32,4224]{2,1,0:T(8,128)(2,1)} %bitcast.80), channel_id=1, source_target_pairs={{0,4},{1,3},{2,6},{3,1},{4,0},{5,7},{6,2},{7,5},{8,12},{9,11},{10,... | collective-permute-start | bytes 3244040 | tf_op jit(solution)/shard_map/ppermute | solution.py:73
  45.0 371.1 %reduce-scatter.6.cloned.1.call-start = ((), (), s32[]{:S(2)}) async-start(), calls=%async_computation.4 | async-start | bytes 1310720 | tf_op jit(solution)/shard_map/reduce_scatter | solution.py:98
  72.5 30.5 %collective-permute-start.4 = (bf16[4,32,4096]{2,1,0:T(8,128)(2,1)}, bf16[4,32,4096]{2,1,0:T(8,128)(2,1)}, u32[]{:S(2)}, u32[]{:S(2)}) collective-permute-start(bf16[4,32,4096]{2,1,0:T(8,128)(2,1)} %bitcast.83), channel_id=1, source_target_pairs={{0,4},{1,3},{2,6},{3,1},{4,0},{5,7},{6,2},{7,5},{8,12},{9,11},{10,... | collective-permute-start | bytes 3145736 | tf_op jit(solution)/shard_map/ppermute | solution.py:73
  75.4 32.2 %copy-start = (bf16[2,4,32,4224]{3,2,1,0:T(8,128)(2,1)}, bf16[2,4,32,4224]{3,2,1,0:T(8,128)(2,1)S(1)}, u32[]{:S(2)}) copy-start(bf16[2,4,32,4224]{3,2,1,0:T(8,128)(2,1)S(1)} %pad_maximum_fusion.p0) | copy-start | bytes 6488068
  75.4 55.4 %collective-permute-start.1 = (bf16[2,4,32,4224]{3,2,1,0:T(8,128)(2,1)S(1)}, bf16[2,4,32,4224]{3,2,1,0:T(8,128)(2,1)}, u32[]{:S(2)}, u32[]{:S(2)}) collective-permute-start(bf16[2,4,32,4224]{3,2,1,0:T(8,128)(2,1)S(1)} %pad_maximum_fusion.p0), channel_id=1, source_target_pairs={{0,2},{1,5},{2,0},{3,7},{4,6},{5,1},{6,4},{7,3},{8,10},{9,13},{10,... | collective-permute-start | bytes 6488072 | tf_op jit(solution)/shard_map/ppermute | solution.py:75
  101.5 26.3 %collective-permute-start.8 = (bf16[4,128,1024]{2,1,0:T(8,128)(2,1)}, bf16[4,128,1024]{2,1,0:T(8,128)(2,1)S(1)}, u32[]{:S(2)}, u32[]{:S(2)}) collective-permute-start(bf16[4,128,1024]{2,1,0:T(8,128)(2,1)} %bitcast.85), channel_id=1, source_target_pairs={{0,4},{1,3},{2,6},{3,1},{4,0},{5,7},{6,2},{7,5},{8,12},{9,11},{10,... | collective-permute-start | bytes 3145736 | tf_op jit(solution)/shard_map/ppermute | solution.py:73
  103.0 24.8 %copy-start.8 = (bf16[512,1024]{1,0:T(8,128)(2,1)S(1)}, bf16[512,1024]{1,0:T(8,128)(2,1)}, u32[]{:S(2)}) copy-start(bf16[512,1024]{1,0:T(8,128)(2,1)} %all-gather.11.cloned.1.call-done) | copy-start | bytes 3145732
  106.1 37.1 %collective-permute-start.5 = (bf16[2,4,32,4096]{3,2,1,0:T(8,128)(2,1)}, bf16[2,4,32,4096]{3,2,1,0:T(8,128)(2,1)}, u32[]{:S(2)}, u32[]{:S(2)}) collective-permute-start(bf16[2,4,32,4096]{3,2,1,0:T(8,128)(2,1)} %pad_maximum_fusion.1.p0.u0), channel_id=1, source_target_pairs={{0,2},{1,5},{2,0},{3,7},{4,6},{5,1},{6,4},{7,3},{8,10},{9,13},{10,... | collective-permute-start | bytes 6291464 | tf_op jit(solution)/shard_map/ppermute | solution.py:75
  107.6 59.2 %collective-permute-start.2 = (bf16[2,4,32,4224]{3,2,1,0:T(8,128)(2,1)S(1)}, bf16[2,4,32,4224]{3,2,1,0:T(8,128)(2,1)}, u32[]{:S(2)}, u32[]{:S(2)}) collective-permute-start(bf16[2,4,32,4224]{3,2,1,0:T(8,128)(2,1)S(1)} %pad_maximum_fusion.p0), channel_id=1, source_target_pairs={{0,1},{1,0},{2,3},{3,2},{4,5},{5,4},{6,7},{7,6},{8,9},{9,8},{10,11... | collective-permute-start | bytes 6488072 | tf_op jit(solution)/shard_map/ppermute | solution.py:76
  127.8 39.5 %copy-start.6 = (bf16[1,512,1024]{2,1,0:T(8,128)(2,1)S(1)}, bf16[1,512,1024]{2,1,0:T(8,128)(2,1)}, u32[]{:S(2)}) copy-start(bf16[1,512,1024]{2,1,0:T(8,128)(2,1)} %param.21) | copy-start | bytes 3145732
  129.3 36.3 %collective-permute-start.9 = (bf16[2,4,128,1024]{3,2,1,0:T(8,128)(2,1)}, bf16[2,4,128,1024]{3,2,1,0:T(8,128)(2,1)}, u32[]{:S(2)}, u32[]{:S(2)}) collective-permute-start(bf16[2,4,128,1024]{3,2,1,0:T(8,128)(2,1)} %pad_maximum_fusion.2.p0), channel_id=1, source_target_pairs={{0,2},{1,5},{2,0},{3,7},{4,6},{5,1},{6,4},{7,3},{8,10},{9,13},{10,... | collective-permute-start | bytes 6291464 | tf_op jit(solution)/shard_map/ppermute | solution.py:75
  130.8 37.7 %collective-permute-start.3 = (bf16[2,4,32,4224]{3,2,1,0:T(8,128)(2,1)}, bf16[2,4,32,4224]{3,2,1,0:T(8,128)(2,1)}, u32[]{:S(2)}, u32[]{:S(2)}) collective-permute-start(bf16[2,4,32,4224]{3,2,1,0:T(8,128)(2,1)} %collective-permute-done.1.p1), channel_id=1, source_target_pairs={{0,1},{1,0},{2,3},{3,2},{4,5},{5,4},{6,7},{7,6},{8,9},{9,8},{10,11... | collective-permute-start | bytes 6488072 | tf_op jit(solution)/shard_map/ppermute | solution.py:76
  130.8 69.2 %collective-permute-start.6 = (bf16[2,4,32,4096]{3,2,1,0:T(8,128)(2,1)}, bf16[2,4,32,4096]{3,2,1,0:T(8,128)(2,1)}, u32[]{:S(2)}, u32[]{:S(2)}) collective-permute-start(bf16[2,4,32,4096]{3,2,1,0:T(8,128)(2,1)} %pad_maximum_fusion.1.p0.u0), channel_id=1, source_target_pairs={{0,1},{1,0},{2,3},{3,2},{4,5},{5,4},{6,7},{7,6},{8,9},{9,8},{10,11... | collective-permute-start | bytes 6291464 | tf_op jit(solution)/shard_map/ppermute | solution.py:76
  143.2 56.8 %collective-permute-start.7 = (bf16[2,4,32,4096]{3,2,1,0:T(8,128)(2,1)}, bf16[2,4,32,4096]{3,2,1,0:T(8,128)(2,1)}, u32[]{:S(2)}, u32[]{:S(2)}) collective-permute-start(bf16[2,4,32,4096]{3,2,1,0:T(8,128)(2,1)} %collective-permute-done.5.p1.u1), channel_id=1, source_target_pairs={{0,1},{1,0},{2,3},{3,2},{4,5},{5,4},{6,7},{7,6},{8,9},{9,8},{10,11... | collective-permute-start | bytes 6291464 | tf_op jit(solution)/shard_map/ppermute | solution.py:76
  165.7 53.1 %collective-permute-start.10 = (bf16[2,4,128,1024]{3,2,1,0:T(8,128)(2,1)}, bf16[2,4,128,1024]{3,2,1,0:T(8,128)(2,1)S(1)}, u32[]{:S(2)}, u32[]{:S(2)}) collective-permute-start(bf16[2,4,128,1024]{3,2,1,0:T(8,128)(2,1)} %pad_maximum_fusion.2.p0), channel_id=1, source_target_pairs={{0,1},{1,0},{2,3},{3,2},{4,5},{5,4},{6,7},{7,6},{8,9},{9,8},{10,11... | collective-permute-start | bytes 6291464 | tf_op jit(solution)/shard_map/ppermute | solution.py:76
  166.8 52.0 %collective-permute-start.11 = (bf16[2,4,128,1024]{3,2,1,0:T(8,128)(2,1)}, bf16[2,4,128,1024]{3,2,1,0:T(8,128)(2,1)S(1)}, u32[]{:S(2)}, u32[]{:S(2)}) collective-permute-start(bf16[2,4,128,1024]{3,2,1,0:T(8,128)(2,1)} %collective-permute-done.9.p1), channel_id=1, source_target_pairs={{0,1},{1,0},{2,3},{3,2},{4,5},{5,4},{6,7},{7,6},{8,9},{9,8},{10,11... | collective-permute-start | bytes 6291464 | tf_op jit(solution)/shard_map/ppermute | solution.py:76
  218.8 1.3 copy-start.14
  218.8 2.0 copy-start.15
  241.5 42.7 %collective-permute-start.15 = (bf16[2,2,4,32,4096]{4,3,2,1,0:T(8,128)(2,1)}, bf16[2,2,4,32,4096]{4,3,2,1,0:T(8,128)(2,1)}, u32[]{:S(2)}, u32[]{:S(2)}) collective-permute-start(bf16[2,2,4,32,4096]{4,3,2,1,0:T(8,128)(2,1)} %get-tuple-element.45), channel_id=1, source_target_pairs={{0,1},{1,0},{2,3},{3,2},{4,5},{5,4},{6,7},{7,6},{8,9},{9,8},{10,11... | collective-permute-start | bytes 12582920 | tf_op jit(solution)/shard_map/ppermute | solution.py:92
  273.6 10.6 %copy-start.2 = (bf16[2,2,4,32,4096]{4,3,2,1,0:T(8,128)(2,1)S(1)}, bf16[2,2,4,32,4096]{4,3,2,1,0:T(8,128)(2,1)}, u32[]{:S(2)}) copy-start(bf16[2,2,4,32,4096]{4,3,2,1,0:T(8,128)(2,1)} %get-tuple-element.44) | copy-start | bytes 12582916
  283.6 11.2 %collective-permute-start.12 = (bf16[2,2,4,32,4096]{4,3,2,1,0:T(8,128)(2,1)}, bf16[2,2,4,32,4096]{4,3,2,1,0:T(8,128)(2,1)S(1)}, u32[]{:S(2)}, u32[]{:S(2)}) collective-permute-start(bf16[2,2,4,32,4096]{4,3,2,1,0:T(8,128)(2,1)} %get-tuple-element.43), channel_id=1, source_target_pairs={{0,1},{1,0},{2,3},{3,2},{4,5},{5,4},{6,7},{7,6},{8,9},{9,8},{10,11... | collective-permute-start | bytes 12582920 | tf_op jit(solution)/shard_map/ppermute | solution.py:92
  283.9 68.9 %collective-permute-start.18 = (bf16[2,2,4,128,1024]{4,3,2,1,0:T(8,128)(2,1)}, bf16[2,2,4,128,1024]{4,3,2,1,0:T(8,128)(2,1)}, u32[]{:S(2)}, u32[]{:S(2)}) collective-permute-start(bf16[2,2,4,128,1024]{4,3,2,1,0:T(8,128)(2,1)} %get-tuple-element.47), channel_id=1, source_target_pairs={{0,1},{1,0},{2,3},{3,2},{4,5},{5,4},{6,7},{7,6},{8,9},{9,8},{10,11... | collective-permute-start | bytes 12582920 | tf_op jit(solution)/shard_map/ppermute | solution.py:92
  284.2 10.6 %copy-start.1 = (bf16[2,2,4,32,4096]{4,3,2,1,0:T(8,128)(2,1)S(1)}, bf16[2,2,4,32,4096]{4,3,2,1,0:T(8,128)(2,1)}, u32[]{:S(2)}) copy-start(bf16[2,2,4,32,4096]{4,3,2,1,0:T(8,128)(2,1)} %get-tuple-element.42) | copy-start | bytes 12582916
  286.7 26.1 %collective-permute-start.16 = (bf16[2,4,32,4096]{3,2,1,0:T(8,128)(2,1)S(1)}, bf16[2,4,32,4096]{3,2,1,0:T(8,128)(2,1)S(1)}, u32[]{:S(2)}, u32[]{:S(2)}) collective-permute-start(bf16[2,4,32,4096]{3,2,1,0:T(8,128)(2,1)S(1)} %fusion.1), channel_id=1, source_target_pairs={{0,4},{1,3},{2,6},{3,1},{4,0},{5,7},{6,2},{7,5},{8,12},{9,11},{10,... | collective-permute-start | bytes 6291464 | tf_op jit(solution)/shard_map/ppermute | solution.py:94
  294.8 51.7 %copy-start.3 = (bf16[2,2,4,32,4096]{4,3,2,1,0:T(8,128)(2,1)}, bf16[2,2,4,32,4096]{4,3,2,1,0:T(8,128)(2,1)S(1)}, u32[]{:S(2)}) copy-start(bf16[2,2,4,32,4096]{4,3,2,1,0:T(8,128)(2,1)S(1)} %collective-permute-done.12) | copy-start | bytes 12582916
  295.6 50.9 %collective-permute-start.13 = (bf16[2,4,32,4096]{3,2,1,0:T(8,128)(2,1)S(1)}, bf16[2,4,32,4096]{3,2,1,0:T(8,128)(2,1)S(1)}, u32[]{:S(2)}, u32[]{:S(2)}) collective-permute-start(bf16[2,4,32,4096]{3,2,1,0:T(8,128)(2,1)S(1)} %fusion), channel_id=1, source_target_pairs={{0,4},{1,3},{2,6},{3,1},{4,0},{5,7},{6,2},{7,5},{8,12},{9,11},{10,... | collective-permute-start | bytes 6291464 | tf_op jit(solution)/shard_map/ppermute | solution.py:94
  314.5 35.1 %collective-permute-start.17 = (bf16[4,32,4096]{2,1,0:T(8,128)(2,1)S(1)}, bf16[4,32,4096]{2,1,0:T(8,128)(2,1)S(1)}, u32[]{:S(2)}, u32[]{:S(2)}) collective-permute-start(bf16[4,32,4096]{2,1,0:T(8,128)(2,1)S(1)} %fusion.6), channel_id=1, source_target_pairs={{0,2},{1,5},{2,0},{3,7},{4,6},{5,1},{6,4},{7,3},{8,10},{9,13},{10,... | collective-permute-start | bytes 3145736 | tf_op jit(solution)/shard_map/ppermute | solution.py:96
  346.6 1.7 copy-start.4
  348.2 20.2 %collective-permute-start.14 = (bf16[4,32,4096]{2,1,0:T(8,128)(2,1)}, bf16[4,32,4096]{2,1,0:T(8,128)(2,1)S(1)}, u32[]{:S(2)}, u32[]{:S(2)}) collective-permute-start(bf16[4,32,4096]{2,1,0:T(8,128)(2,1)} %fusion.9), channel_id=1, source_target_pairs={{0,2},{1,5},{2,0},{3,7},{4,6},{5,1},{6,4},{7,3},{8,10},{9,13},{10,... | collective-permute-start | bytes 3145736 | tf_op jit(solution)/shard_map/ppermute | solution.py:96
  352.6 66.0 %reduce-scatter.4.cloned.1.call-start = ((), (), s32[]{:S(2)}) async-start(), calls=%async_computation.3 | async-start | bytes 1310720 | tf_op jit(solution)/shard_map/reduce_scatter | solution.py:98
  352.8 15.5 %copy-start.5 = (bf16[2,4,32,4096]{3,2,1,0:T(8,128)(2,1)S(1)}, bf16[2,4,32,4096]{3,2,1,0:T(8,128)(2,1)}, u32[]{:S(2)}) copy-start(bf16[2,4,32,4096]{3,2,1,0:T(8,128)(2,1)} %copy-done.4) | copy-start | bytes 6291460
  356.3 28.0 %collective-permute-start.19 = (bf16[2,4,128,1024]{3,2,1,0:T(8,128)(2,1)S(1)}, bf16[2,4,128,1024]{3,2,1,0:T(8,128)(2,1)}, u32[]{:S(2)}, u32[]{:S(2)}) collective-permute-start(bf16[2,4,128,1024]{3,2,1,0:T(8,128)(2,1)S(1)} %fusion.2), channel_id=1, source_target_pairs={{0,4},{1,3},{2,6},{3,1},{4,0},{5,7},{6,2},{7,5},{8,12},{9,11},{10,... | collective-permute-start | bytes 6291464 | tf_op jit(solution)/shard_map/ppermute | solution.py:94
  371.6 62.9 %reduce-scatter.8.cloned.1.call-start = ((), (), s32[]{:S(2)}) async-start(), calls=%async_computation.5 | async-start | bytes 1310720 | tf_op jit(solution)/shard_map/reduce_scatter | solution.py:98
  386.9 14.9 %collective-permute-start.20 = (bf16[4,128,1024]{2,1,0:T(8,128)(2,1)S(1)}, bf16[4,128,1024]{2,1,0:T(8,128)(2,1)S(1)}, u32[]{:S(2)}, u32[]{:S(2)}) collective-permute-start(bf16[4,128,1024]{2,1,0:T(8,128)(2,1)S(1)} %fusion.3), channel_id=1, source_target_pairs={{0,2},{1,5},{2,0},{3,7},{4,6},{5,1},{6,4},{7,3},{8,10},{9,13},{10,... | collective-permute-start | bytes 3145736 | tf_op jit(solution)/shard_map/ppermute | solution.py:96
  405.6 10.5 %copy-start.7 = (bf16[32,4096]{1,0:T(8,128)(2,1)S(1)}, bf16[32,4096]{1,0:T(8,128)(2,1)}, u32[]{:S(2)}) copy-start(bf16[32,4096]{1,0:T(8,128)(2,1)} %param.17) | copy-start | bytes 786436
  405.6 12.4 %copy-start.16 = (bf16[32]{0:T(256)(128)(2,1)S(1)}, bf16[32]{0:T(256)(128)(2,1)}, u32[]{:S(2)}) copy-start(bf16[32]{0:T(256)(128)(2,1)} %param.20) | copy-start | bytes 196
  405.6 13.9 %copy-start.10 = (bf16[32,1024]{1,0:T(8,128)(2,1)S(1)}, bf16[32,1024]{1,0:T(8,128)(2,1)}, u32[]{:S(2)}) copy-start(bf16[32,1024]{1,0:T(8,128)(2,1)} %param.13) | copy-start | bytes 196612
  405.6 13.9 %copy-start.11 = (bf16[32,1024]{1,0:T(8,128)(2,1)S(1)}, bf16[32,1024]{1,0:T(8,128)(2,1)}, u32[]{:S(2)}) copy-start(bf16[32,1024]{1,0:T(8,128)(2,1)} %param.14) | copy-start | bytes 196612
  405.6 13.9 %copy-start.12 = (bf16[32,1024]{1,0:T(8,128)(2,1)S(1)}, bf16[32,1024]{1,0:T(8,128)(2,1)}, u32[]{:S(2)}) copy-start(bf16[32,1024]{1,0:T(8,128)(2,1)} %param.15) | copy-start | bytes 196612
  416.0 4.5 %copy-start.13 = (bf16[32]{0:T(256)(128)(2,1)S(1)}, bf16[32]{0:T(256)(128)(2,1)}, u32[]{:S(2)}) copy-start(bf16[32]{0:T(256)(128)(2,1)} %param.19) | copy-start | bytes 196
Sparse Core Ops, SparseCore 0:
  12.3 31.1 all-gather.6
  45.0 27.4 all-gather.8
  74.1 27.4 all-gather.10
  352.7 25.7 reduce-scatter.5
  380.7 25.8 reduce-scatter.3
  408.7 25.7 reduce-scatter.7
